TPU v7x, 512 devices: a whole 4x8x8 slice. The times are simulated.
512 devices in a mesh: ctx: 64 (over z_lo, y, x), head: 8 (over z_hi, core).
Axes of the slice: x: 4, y: 8, z: 8 (z_hi: 4, z_lo: 2; z = z_hi * 2 + z_lo), core: 2. Of those that a mesh axis runs over, the one named last changes fastest.
Arguments:
- queries: bfloat16 [8192, 2048], P('ctx', 'head'), may hold values from -6 to 6
- key_rows: bfloat16 [8192, 128], P('ctx'), may hold values from -6 to 6
- value_rows: bfloat16 [8192, 128], P('ctx'), may hold values from -6 to 6
- out_grad: bfloat16 [8192, 2048], P('ctx', 'head'), may hold values from -6 to 6
- doc_lengths: int32 [8], replicated, may hold values from 1 to 4096, 8192 in all
- span_order: int32 [64, 2], replicated, may hold values from 0 to 127, as said below
Outputs:
- query_grad: bfloat16 [8192, 2048], P('ctx', 'head')
- key_grad: bfloat16 [8192, 128], P(('ctx', 'head'))
- value_grad: bfloat16 [8192, 128], P(('ctx', 'head'))
Inputs may be any that keep to these rules, and one draw needn't show every extreme that they name: `doc_lengths`: the lengths sum to 8192; the longest is exactly 4096. `span_order`: row i holds a span number c and its mirror 128 - 1 - c, in that order; the first entries of all rows are distinct.
All inputs are finite; a program needn't handle non-finite values.
Results may differ from a plain program's by a relative error of at most 0.025.
Values may be sent and summed in bfloat16 or wider, within the bound.
A program may use at most 64 MiB of HBM per device.

v0:
```python
import jax
import jax.numpy as jnp
from jax import lax
from jax.sharding import PartitionSpec as P

masked_value = -1e30


def local(queries, key_rows, value_rows, out_grad, doc_lengths, span_order):
    local_rows = queries.shape[0]
    head_dim = key_rows.shape[1]
    local_heads = queries.shape[1] // head_dim
    ctx_size = lax.axis_size("ctx")
    total_rows = local_rows * ctx_size
    span_rows = local_rows // 2
    positions = (
        span_order.reshape(-1)[:, None] * span_rows
        + jnp.arange(span_rows, dtype=jnp.int32)[None, :]
    ).reshape(-1)
    starts = jnp.cumsum(doc_lengths) - doc_lengths
    documents = jnp.sum((starts[None, :] <= positions[:, None]).astype(jnp.int32), axis=1) - 1
    ctx_index = lax.axis_index("ctx")
    own_pos = lax.dynamic_slice_in_dim(positions, ctx_index * local_rows, local_rows)
    own_doc = lax.dynamic_slice_in_dim(documents, ctx_index * local_rows, local_rows)
    all_keys, all_values = (
        lax.all_gather(key_rows, "ctx", axis=0, tiled=True),
        lax.all_gather(value_rows, "ctx", axis=0, tiled=True),
    )
    scaling = head_dim ** (-0.5)
    query_heads = queries.reshape(local_rows, local_heads, head_dim)
    grad_heads = out_grad.reshape(local_rows, local_heads, head_dim)
    width = min(512, total_rows)
    blocks = total_rows // width

    def block_data(index):
        start = index * width
        key_block = lax.dynamic_slice_in_dim(all_keys, start, width)
        value_block = lax.dynamic_slice_in_dim(all_values, start, width)
        key_pos = lax.dynamic_slice_in_dim(positions, start, width)
        key_doc = lax.dynamic_slice_in_dim(documents, start, width)
        allowed = (own_doc[:, None] == key_doc[None, :]) & (key_pos[None, :] <= own_pos[:, None])
        return (key_block, value_block, allowed)

    def products(key_block, value_block):
        scores = (
            jnp.einsum("qhd,kd->hqk", query_heads, key_block, preferred_element_type=jnp.float32)
            * scaling
        )
        dprobs = jnp.einsum(
            "qhd,kd->hqk", grad_heads, value_block, preferred_element_type=jnp.float32
        )
        return (scores, dprobs)

    def gather_stats(index, carry):
        key_block, value_block, allowed = block_data(index)
        run_max, run_sum, run_dot = carry
        scores, dprobs = products(key_block, value_block)
        masked = jnp.where(allowed[None], scores, masked_value)
        new_max = jnp.maximum(run_max, jnp.max(masked, axis=-1))
        expo = jnp.where(allowed[None], jnp.exp(masked - new_max[..., None]), 0.0)
        rescale = jnp.exp(run_max - new_max)
        return (
            new_max,
            run_sum * rescale + jnp.sum(expo, axis=-1),
            run_dot * rescale + jnp.sum(expo * dprobs, axis=-1),
        )

    start_stats = (
        jnp.full((local_heads, local_rows), masked_value, jnp.float32),
        jnp.zeros((local_heads, local_rows), jnp.float32),
        jnp.zeros((local_heads, local_rows), jnp.float32),
    )
    run_max, run_sum, run_dot = lax.fori_loop(0, blocks, gather_stats, start_stats)
    log_total = run_max + jnp.log(run_sum)
    row_delta = run_dot / run_sum

    def backward(dq_total, index):
        key_block, value_block, allowed = block_data(index)
        total = dq_total
        scores, dprobs = products(key_block, value_block)
        masked = jnp.where(allowed[None], scores, masked_value)
        weights = jnp.where(allowed[None], jnp.exp(masked - log_total[..., None]), 0.0)
        weights_low = weights.astype(jnp.bfloat16)
        dscores = (weights * (dprobs - row_delta[..., None])).astype(jnp.bfloat16)
        value_part = jnp.einsum(
            "hqk,qhd->kd", weights_low, grad_heads, preferred_element_type=jnp.float32
        )
        key_part = (
            jnp.einsum("hqk,qhd->kd", dscores, query_heads, preferred_element_type=jnp.float32)
            * scaling
        )
        total = total + jnp.einsum(
            "hqk,kd->qhd", dscores, key_block, preferred_element_type=jnp.float32
        )
        return (total, jnp.concatenate([key_part, value_part], axis=1))

    dq_total, pieces = lax.scan(
        backward, jnp.zeros((local_rows, local_heads, head_dim), jnp.float32), jnp.arange(blocks)
    )
    query_grad = (
        (dq_total * scaling).reshape(local_rows, local_heads * head_dim).astype(jnp.bfloat16)
    )
    partial_value = pieces.reshape(total_rows, 2 * head_dim)
    terms = partial_value.reshape(ctx_size, local_rows, 2 * head_dim)
    terms = lax.all_to_all(
        terms.astype(jnp.bfloat16), "ctx", split_axis=0, concat_axis=0, tiled=True
    ).astype(terms.dtype)
    owned = jnp.sum(terms, axis=0)
    summed = lax.psum_scatter(
        owned.astype(jnp.bfloat16), "head", scatter_dimension=0, tiled=True
    ).astype(jnp.float32)
    key_grad = summed[:, :head_dim].astype(jnp.bfloat16)
    value_grad = summed[:, head_dim:].astype(jnp.bfloat16)
    return (query_grad, key_grad, value_grad)


def solution(mesh):
    in_specs = (P("ctx", "head"), P("ctx", None), P("ctx", None), P("ctx", "head"), P(), P())
    out_specs = (P("ctx", "head"), P(("ctx", "head"), None), P(("ctx", "head"), None))
    return jax.shard_map(local, mesh=mesh, in_specs=in_specs, out_specs=out_specs, check_vma=False)
```

profile of v0, /device:TPU:6, one launch (start us, length us, event | category | flops | bytes accessed | tf_op | source)
XLA Modules:
  0.0 877.2 jit_solution(3569151629039220598)
XLA Ops:
  13.8 297.4 %all-gather.3.cloned.1.call-done = bf16[8192,128]{1,0:T(8,128)(2,1)} async-done(((bf16[128,128]{1,0:T(8,128)(2,1)}), bf16[8192,128]{1,0:T(8,128)(2,1)}) %all-gather.3.cloned.1.call-update) | async-done | bytes 2097168 | tf_op jit(solution)/shard_map/all_gather | solution.py:26
  311.2 302.0 %all-gather.5.cloned.1.call-done = bf16[8192,128]{1,0:T(8,128)(2,1)} async-done(((bf16[128,128]{1,0:T(8,128)(2,1)}), bf16[8192,128]{1,0:T(8,128)(2,1)}) %all-gather.5.cloned.1.call-update) | async-done | bytes 2097168 | tf_op jit(solution)/shard_map/all_gather | solution.py:27
  613.2 46.7 %while.31 = (s32[]{:T(128)}, f32[2,128]{1,0:T(2,128)S(1)}, f32[2,128]{1,0:T(2,128)S(1)}, f32[2,128]{1,0:T(2,128)S(1)}, s32[128]{0:T(128)S(1)}, /*index=5*/s32[81...) while((s32[]{:T(128)}, f32[2,128]{1,0:T(2,128)S(1)}, ...), condition=%wide.region_6.7_spmd.clone, body=%wide.region_2.6_spmd.clone.sunk | while | flops 68617984 | bytes 2260198 | solution.py:73
  614.7 1.2 fusion.72
  617.7 1.2 fusion.72
  620.6 1.2 fusion.72
  623.5 1.2 fusion.72
  626.4 1.2 fusion.72
  629.4 1.2 fusion.72
  632.3 1.2 fusion.72
  635.2 1.2 fusion.72
  638.1 1.2 fusion.72
  641.1 1.2 fusion.72
  644.0 1.2 fusion.72
  646.9 1.2 fusion.72
  649.8 1.2 fusion.72
  652.7 1.2 fusion.72
  655.7 1.2 fusion.72
  658.6 1.2 fusion.72
  660.0 103.2 %while.32 = (s32[]{:T(128)}, f32[128,2,128]{0,2,1:T(8,128)S(1)}, bf16[16,512,256]{2,1,0:T(8,128)(2,1)}, s32[16]{0:T(128)S(1)}, bf16[8192,128]{1,0:T(8,128)(2,1)}...) while((s32[]{:T(128)}, f32[128,2,128]{0,2,1:T(8,128)S(1)}, ...), condition=%wide.region_8.9_spmd.clone, body=%wide.region_7.8_spmd.clone.sunk | while | flops 169738240 | bytes 5258505 | solution.py:97
  763.2 66.1 %all_to_all.5 = bf16[64,128,256]{2,1,0:T(8,128)(2,1)} all-to-all(bf16[64,128,256]{2,1,0:T(8,128)(2,1)} %bitcast.117), channel_id=1, replica_groups=mesh['ctx'=64,'head'=8] {'ctx'}, dimensions={0} | all-to-all | bytes 8388608 | tf_op jit(solution)/shard_map/all_to_all | solution.py:105
  829.3 3.4 reduce_sum.48
  833.6 35.8 %reduce-scatter.2.cloned.1.call-done = bf16[16,256]{1,0:T(8,128)(2,1)} async-done(((bf16[128,256]{1,0:T(8,128)(2,1)}), bf16[16,256]{1,0:T(8,128)(2,1)}) %reduce-scatter.2.cloned.1.call-update) | async-done | bytes 8208 | tf_op jit(solution)/shard_map/reduce_scatter | solution.py:109
  869.4 1.3 fusion.35
  (350 shorter events, 125.8 us)
Async XLA Ops:
  7.2 304.1 %all-gather.3.cloned.1.call-start = ((), (), s32[]{:S(2)}) async-start(), calls=%async_computation.2 | async-start | bytes 2129920 | tf_op jit(solution)/shard_map/all_gather | solution.py:26
  7.9 605.3 %all-gather.5.cloned.1.call-start = ((), (), s32[]{:S(2)}) async-start(), calls=%async_computation.3 | async-start | bytes 2129920 | tf_op jit(solution)/shard_map/all_gather | solution.py:27
  8.6 860.8 %reduce-scatter.2.cloned.1.call-start = ((), (), s32[]{:S(2)}) async-start(), calls=%async_computation.4 | async-start | bytes 73728 | tf_op jit(solution)/shard_map/reduce_scatter | solution.py:109
Sparse Core Ops, SparseCore 0:
  10.1 301.1 all-gather.2
  313.3 299.8 all-gather.4
  832.9 36.4 reduce-scatter.1
where the time goes:
time: 879 us; the launch traced here: 877 us
  waiting for transfers between devices  637 us (72%)
  matrix products  100 us (11%)
  blocking collectives  66.1 us (8%)
  local copies, waits for them, and re-layouts  32.7 us (4%)
  other arithmetic  15.1 us (2%)
  between operations  13.9 us (2%)
  loops' own time  12.4 us (1%)
    all_gather x1, waiting for transfers between devices, local(): lax.all_gather(value_rows, 'ctx', axis=0, tiled=True)  302 us
    all_gather x1, waiting for transfers between devices, local(): lax.all_gather(key_rows, 'ctx', axis=0, tiled=True)  297 us
    all_to_all x1, blocking collectives, local(): lax.all_to_all(terms.astype(jnp.bfloat16), 'ctx', split_axis=0, concat_ax...  66.1 us
    dot_general x32, matrix products, products(): jnp.einsum('qhd,kd->hqk', query_heads, key_block, preferred_element_type=...  37.5 us
    dot_general x32, matrix products, products(): jnp.einsum('qhd,kd->hqk', grad_heads, value_block, preferred_element_type...  37 us
    reduce_scatter x1, waiting for transfers between devices, local(): lax.psum_scatter(owned.astype(jnp.bfloat16), 'head', scatter_dimension=0,...  35.8 us
    dot_general x16, matrix products, backward(): jnp.einsum('hqk,kd->qhd', dscores, key_block, preferred_element_type=jnp....  18.6 us
  transfers between devices with their start and end apart: 3, of which 3 were waited for; matrix products, arithmetic and copies ran while one was open for 1% of the time, Pallas kernels for 0%

commit v1 on v0

v1 whole, which is shorter than its diff:
```python
import functools
import math

import jax
import jax.numpy as jnp
from jax import lax
from jax.experimental import pallas as pl
from jax.experimental.pallas import tpu as pltpu
from jax.sharding import PartitionSpec as P

MESH = pl.DeviceIdType.MESH
F32 = jnp.float32
BF16 = jnp.bfloat16
NX, NY, NZH = 4, 8, 4
HD = 128
NEG = -1e30
SCALE = HD ** -0.5
EXP_SCALE = SCALE / math.log(2.0)
CK = 512
UQ = 256


def kernel(
    lens_ref, order_ref, q_ref, g_ref, k_ref, v_ref,
    dq_ref, dk_ref, dv_ref,
    kv, qa, ga, qs, gs, kp, qlim, es, dps, ws, dss, dqa, pf, st, rst, lim,
    dqb, dqr, sb, m1, rr, rl, yb, yr, zb, zr,
    lsem, qsend, qrecv, ysend, yrecv, xsend, xrecv, ssend, srecv, dsend, drecv,
    m1send, m1recv, rsend, rrecv, lsend, lrecv, rysend, ryrecv, zsend, zrecv,
):
    ctx = lax.axis_index("ctx")
    head = lax.axis_index("head")
    zl, y, x = ctx // 32, (ctx // 4) % 8, ctx % 4
    zh, core = head // 2, head % 2

    def at(zl_, y_, x_):
        return zl_ * 32 + y_ * 4 + x_

    right = (at(zl, y, (x + 1) % 4), head)
    left = (at(zl, y, (x + 3) % 4), head)
    ydev = [(at(zl, (y + r) % 8, x), head) for r in range(8)]
    zdev = [(ctx, ((zh + r) % 4) * 2 + core) for r in range(4)]
    gdev = [
        (at((zl + k // 2) % 2, y, x), zh * 2 + (core + k % 2) % 2) for k in range(4)
    ]

    stage = [
        pltpu.make_async_copy(k_ref.at[:, core], kv.at[0, x, y], lsem.at[0]),
        pltpu.make_async_copy(v_ref.at[:, core], kv.at[1, x, y], lsem.at[1]),
        pltpu.make_async_copy(q_ref, qa.at[0], lsem.at[2]),
        pltpu.make_async_copy(g_ref, ga.at[0], lsem.at[3]),
    ]
    for c in stage:
        c.start()

    barrier = pltpu.get_barrier_semaphore()
    peers = [right, left] + ydev[1:] + zdev[1:] + gdev[1:]
    for p in peers:
        pl.semaphore_signal(barrier, inc=1, device_id=p, device_id_type=MESH)
    pl.semaphore_wait(barrier, len(peers))

    pending = []

    def send(src, dst, ss, rs, dev):
        c = pltpu.make_async_remote_copy(
            src_ref=src, dst_ref=dst, send_sem=ss, recv_sem=rs,
            device_id=dev, device_id_type=MESH,
        )
        c.start()
        pending.append(c)
        return c

    def arrival(dst, ss, rs):
        return pltpu.make_async_remote_copy(
            src_ref=dst, dst_ref=dst, send_sem=ss, recv_sem=rs,
            device_id=right, device_id_type=MESH,
        )

    stage[0].wait()
    stage[1].wait()

    def blk(xr, yr_):
        return kv.at[:, (x + xr) % 4, (y + yr_) % 8]

    def x_forward(r):
        b = blk(0, r)
        send(b, b, xsend.at[r, 0], xrecv.at[r, 0], right)
        send(b, b, xsend.at[r, 1], xrecv.at[r, 1], left)

    def y_send(r, up):
        b = blk(0, r)
        i = (-r) % 8 if up else r
        j = i if up else 4 + i
        dev = ydev[1] if up else ydev[7]
        send(b, b, ysend.at[j], yrecv.at[j], dev)

    y_send(0, True)
    y_send(0, False)
    x_forward(0)
    for k in range(1, 4):
        send(q_ref, qa.at[k], qsend.at[k, 0], qrecv.at[k, 0], gdev[k])
        send(g_ref, ga.at[k], qsend.at[k, 1], qrecv.at[k, 1], gdev[k])

    def x_arrive(r):
        bl, br = blk(3, r), blk(1, r)
        arrival(bl, xsend.at[r, 0], xrecv.at[r, 0]).wait_recv()
        if r % 2 == 0:
            send(bl, bl, xsend.at[r, 2], xrecv.at[r, 2], right)
        arrival(br, xsend.at[r, 1], xrecv.at[r, 1]).wait_recv()
        if r % 2 == 1:
            send(br, br, xsend.at[r, 2], xrecv.at[r, 2], left)

    prev = [0]
    for d in range(1, 5):
        r = -d
        b = blk(0, r)
        arrival(b, ysend.at[d - 1], yrecv.at[d - 1]).wait_recv()
        if d < 4:
            y_send(r, True)
        x_forward(r % 8)
        got = [r % 8]
        if d < 4:
            r = d
            b = blk(0, r)
            arrival(b, ysend.at[3 + d], yrecv.at[3 + d]).wait_recv()
            if d < 3:
                y_send(r, False)
            x_forward(r)
            got.append(r)
        for p in prev:
            x_arrive(p)
        prev = got
    for p in prev:
        x_arrive(p)
    for r in range(8):
        b = blk(2, r)
        arrival(b, xsend.at[r, 2], xrecv.at[r, 2]).wait_recv()

    stage[2].wait()
    stage[3].wait()
    for k in range(1, 4):
        arrival(qa.at[k], qsend.at[k, 0], qrecv.at[k, 0]).wait_recv()
        arrival(ga.at[k], qsend.at[k, 1], qrecv.at[k, 1]).wait_recv()
    lane = lax.broadcasted_iota(jnp.int32, (8, HD), 1) % 64
    starts = []
    total = jnp.int32(0)
    for i in range(8):
        starts.append(total)
        total = total + lens_ref[i]
    for dz in range(2):
        octx = at((zl + dz) % 2, y, x)
        for h in range(2):
            u = dz * 2 + h
            for dc in range(2):
                for hd in range(2):
                    rows = slice(h * 64, h * 64 + 64)
                    cols = slice(hd * HD, hd * HD + HD)
                    o = (dc * 2 + hd) * 64
                    qs[u, o : o + 64, :] = qa[dz * 2 + dc, rows, cols]
                    gs[u, o : o + 64, :] = ga[dz * 2 + dc, rows, cols]
            qp = order_ref[octx, h] * 64 + lane
            first = jnp.zeros_like(qp)
            for s in starts:
                first = jnp.maximum(first, jnp.where(qp >= s, s, 0))
            qlim[u, 0] = qp
            qlim[u, 1] = first
    row = lax.broadcasted_iota(jnp.int32, (32, HD), 0)
    pattern = (row // 16) * 32 + row % 16 + core * 16
    for xc in range(4):
        for yc in range(8):
            for h in range(2):
                span = order_ref[at(zl, yc, xc), h]
                o = yc * 64 + h * 32
                kp[xc, o : o + 32, :] = pattern + span * 64

    def pass1(i, carry):
        xc, u = i // 4, i % 4
        keys = kv[0, xc].reshape(CK, HD)
        vals = kv[1, xc].reshape(CK, HD)
        dims = (((1,), (1,)), ((), ()))
        s = lax.dot_general(keys, qs[u], dims, preferred_element_type=F32)
        dp = lax.dot_general(vals, gs[u], dims, preferred_element_type=F32)
        dps[xc, u] = dp
        pos = kp[xc]
        allowed = (pos <= qlim[u, 0, 0:1, :]) & (pos >= qlim[u, 1, 0:1, :])
        for dc in range(2):
            cols = slice(dc * HD, dc * HD + HD)
            sh = jnp.where(allowed, s[:, cols], NEG)
            m = jnp.max(sh, axis=0, keepdims=True)
            e = jnp.exp2((sh - m) * EXP_SCALE)
            es[xc, u, :, cols] = e
            lim[xc, u, 0, 0:1, cols] = m
            lim[xc, u, 1, 0:1, cols] = jnp.sum(e, axis=0, keepdims=True)
            lim[xc, u, 2, 0:1, cols] = jnp.sum(e * dp[:, cols], axis=0, keepdims=True)
        return carry

    lax.fori_loop(0, 16, pass1, 0)

    for dz in range(2):
        for h in range(2):
            u = dz * 2 + h
            for dc in range(2):
                cols = slice(dc * HD, dc * HD + HD)
                ms = [lim[xc, u, 0, 0:1, cols] for xc in range(4)]
                m = jnp.maximum(jnp.maximum(ms[0], ms[1]), jnp.maximum(ms[2], ms[3]))
                sc = [jnp.exp2((a - m) * EXP_SCALE) for a in ms]
                k = dz * 2 + dc
                st[0, k, h : h + 1, :] = m
                st[1, k, h : h + 1, :] = sum(sc[c] * lim[c, u, 1, 0:1, cols] for c in range(4))
                st[2, k, h : h + 1, :] = sum(sc[c] * lim[c, u, 2, 0:1, cols] for c in range(4))
    for k in range(1, 4):
        send(st, rst.at[k], ssend.at[k], srecv.at[k], gdev[k])
    for k in range(1, 4):
        arrival(rst.at[k], ssend.at[k], srecv.at[k]).wait_recv()
    for k in range(4):
        ms = [st[0, k]] + [rst[p, 0, k ^ p] for p in range(1, 4)]
        ls = [st[1, k]] + [rst[p, 1, k ^ p] for p in range(1, 4)]
        ds = [st[2, k]] + [rst[p, 2, k ^ p] for p in range(1, 4)]
        m = jnp.maximum(jnp.maximum(ms[0], ms[1]), jnp.maximum(ms[2], ms[3]))
        sc = [jnp.exp2((a - m) * EXP_SCALE) for a in ms]
        inv = 1.0 / (sc[0] * ls[0] + sc[1] * ls[1] + sc[2] * ls[2] + sc[3] * ls[3])
        delta = (sc[0] * ds[0] + sc[1] * ds[1] + sc[2] * ds[2] + sc[3] * ds[3]) * inv
        dz, dc = k // 2, k % 2
        cols = slice(dc * HD, dc * HD + HD)
        for h in range(2):
            u = dz * 2 + h
            for xc in range(4):
                a = jnp.exp2((lim[xc, u, 0, 0:1, cols] - m[h : h + 1, :]) * EXP_SCALE)
                lim[xc, u, 3, 0:1, cols] = a * inv[h : h + 1, :]
            lim[0, u, 4, 0:1, cols] = delta[h : h + 1, :]

    dqa[...] = jnp.zeros_like(dqa)

    def column(c):
        xc = (x + c) % 4

        def unit(u, carry):
            w = es[xc, u] * lim[xc, u, 3, 0:1, :]
            o = pl.multiple_of(u * UQ, UQ)
            ws[:, pl.ds(o, UQ)] = w.astype(BF16)
            dss[:, pl.ds(o, UQ)] = (w * (dps[xc, u] - lim[0, u, 4, 0:1, :])).astype(BF16)
            return carry

        lax.fori_loop(0, 4, unit, 0)
        dims = (((1,), (0,)), ((), ()))
        q_all = qs[...].reshape(4 * UQ, HD)
        g_all = gs[...].reshape(4 * UQ, HD)
        dkc = lax.dot_general(dss[...], q_all, dims, preferred_element_type=F32)
        pf[c, 0] = dkc.reshape(8, 64, HD)
        dvc = lax.dot_general(ws[...], g_all, dims, preferred_element_type=F32)
        pf[c, 1] = dvc.reshape(8, 64, HD)
        keys = kv[0, xc].reshape(CK, HD)
        dqa[...] += lax.dot_general(
            dss[...], keys, (((0,), (0,)), ((), ())), preferred_element_type=F32
        )

    def mine(c, r):
        return pf[c, :, (y + r) % 8]

    order = [4, 3, 5, 2, 6, 1, 7, 0]
    column(2)
    for r in order:
        sb[2, r] = mine(2, r).astype(BF16)
        dev = right if r % 2 == 0 else left
        send(sb.at[2, r], m1.at[r], m1send.at[r], m1recv.at[r], dev)
    column(1)
    for r in order:
        if r % 2 == 1:
            sb[1, r] = mine(1, r).astype(BF16)
            send(sb.at[1, r], rr.at[r], rsend.at[r], rrecv.at[r], right)
    column(3)
    for r in order:
        if r % 2 == 0:
            sb[3, r] = mine(3, r).astype(BF16)
            send(sb.at[3, r], rl.at[r], lsend.at[r], lrecv.at[r], left)
    for r in order:
        arrival(m1.at[r], m1send.at[r], m1recv.at[r]).wait_recv()
        c = 1 if r % 2 == 0 else 3
        sb[c, r] = (mine(c, r) + m1[r].astype(F32)).astype(BF16)
        if r % 2 == 0:
            send(sb.at[1, r], rr.at[r], rsend.at[r], rrecv.at[r], right)
        else:
            send(sb.at[3, r], rl.at[r], lsend.at[r], lrecv.at[r], left)
    column(0)

    for k in range(4):
        dz, dc = k // 2, k % 2
        for h in range(2):
            for hd in range(2):
                o = (dz * 2 + h) * UQ + (dc * 2 + hd) * 64
                rows = slice(h * 64, h * 64 + 64)
                cols = slice(hd * HD, hd * HD + HD)
                part = dqa[o : o + 64, :]
                if k == 0:
                    dq_ref[rows, cols] = part.astype(BF16)
                else:
                    dqb[k, rows, cols] = part.astype(BF16)
        if k > 0:
            send(dqb.at[k], dqr.at[k], dsend.at[k], drecv.at[k], gdev[k])

    own = None
    for r in order:
        arrival(rr.at[r], rsend.at[r], rrecv.at[r]).wait_recv()
        arrival(rl.at[r], lsend.at[r], lrecv.at[r]).wait_recv()
        t = mine(0, r) + rr[r].astype(F32) + rl[r].astype(F32)
        if r == 0:
            own = t
        else:
            yb[r] = t.astype(BF16)
            send(yb.at[r], yr.at[r], rysend.at[r], ryrecv.at[r], ydev[r])
    for k in range(1, 4):
        arrival(dqr.at[k], dsend.at[k], drecv.at[k]).wait_recv()
    for h in range(2):
        for hd in range(2):
            o = h * UQ + hd * 64
            rows = slice(h * 64, h * 64 + 64)
            cols = slice(hd * HD, hd * HD + HD)
            t = dqa[o : o + 64, :]
            for k in range(1, 4):
                t = t + dqr[k, rows, cols].astype(F32)
            dq_ref[rows, cols] = (t * SCALE).astype(BF16)
    for r in (1, 7, 2, 6, 3, 5, 4):
        arrival(yr.at[r], rysend.at[r], ryrecv.at[r]).wait_recv()
        own = own + yr[r].astype(F32)
    pf[0, :, 0] = own
    for r in range(1, 4):
        o = pl.multiple_of(((zh + r) % 4) * 16, 16)
        zb[r] = pf[0, :, 0, pl.ds(o, 16), :].astype(BF16)
        send(zb.at[r], zr.at[r], zsend.at[r], zrecv.at[r], zdev[r])
    fin = pf[0, :, 0, pl.ds(pl.multiple_of(zh * 16, 16), 16), :]
    for r in range(1, 4):
        arrival(zr.at[r], zsend.at[r], zrecv.at[r]).wait_recv()
        fin = fin + zr[r].astype(F32)
    dk_ref[...] = (fin[0] * SCALE).astype(BF16)
    dv_ref[...] = fin[1].astype(BF16)
    for c in pending:
        c.wait_send()


def local(queries, key_rows, value_rows, out_grad, doc_lengths, span_order):
    vm = pltpu.VMEM
    dma = pltpu.SemaphoreType.DMA
    piece = (2, 64, HD)
    scratch = [
        vm((2, NX, NY, 4, 16, HD), BF16),
        vm((4, 128, 256), BF16),
        vm((4, 128, 256), BF16),
        vm((4, UQ, HD), BF16),
        vm((4, UQ, HD), BF16),
        vm((NX, CK, HD), jnp.int32),
        vm((4, 2, 8, HD), jnp.int32),
        vm((NX, 4, CK, UQ), F32),
        vm((NX, 4, CK, UQ), F32),
        vm((CK, 4 * UQ), BF16),
        vm((CK, 4 * UQ), BF16),
        vm((4 * UQ, HD), F32),
        vm((4, 2, 8, 64, HD), F32),
        vm((3, 4, 2, HD), F32),
        vm((4, 3, 4, 2, HD), F32),
        vm((NX, 4, 5, 8, UQ), F32),
        vm((4, 128, 256), BF16),
        vm((4, 128, 256), BF16),
        vm((4, 8) + piece, BF16),
        vm((8,) + piece, BF16),
        vm((8,) + piece, BF16),
        vm((8,) + piece, BF16),
        vm((8,) + piece, BF16),
        vm((8,) + piece, BF16),
        vm((4, 2, 16, HD), BF16),
        vm((4, 2, 16, HD), BF16),
        dma((4,)),
        dma((4, 2)), dma((4, 2)),
        dma((8,)), dma((8,)),
        dma((8, 3)), dma((8, 3)),
        dma((4,)), dma((4,)),
        dma((4,)), dma((4,)),
        dma((8,)), dma((8,)),
        dma((8,)), dma((8,)),
        dma((8,)), dma((8,)),
        dma((8,)), dma((8,)),
        dma((4,)), dma((4,)),
    ]
    smem = pl.BlockSpec(memory_space=pltpu.SMEM)
    hbm = pl.BlockSpec(memory_space=pl.ANY)
    vmem = pl.BlockSpec(memory_space=pltpu.VMEM)
    return pl.pallas_call(
        kernel,
        out_shape=(
            jax.ShapeDtypeStruct((128, 256), BF16),
            jax.ShapeDtypeStruct((16, HD), BF16),
            jax.ShapeDtypeStruct((16, HD), BF16),
        ),
        in_specs=[smem, smem, hbm, hbm, hbm, hbm],
        out_specs=(vmem, vmem, vmem),
        scratch_shapes=scratch,
        compiler_params=pltpu.CompilerParams(
            collective_id=0, has_side_effects=True, vmem_limit_bytes=60 * 1024 * 1024
        ),
    )(
        doc_lengths,
        span_order,
        queries,
        out_grad,
        key_rows.reshape(4, 2, 16, HD),
        value_rows.reshape(4, 2, 16, HD),
    )


def solution(mesh):
    in_specs = (P("ctx", "head"), P("ctx", None), P("ctx", None), P("ctx", "head"), P(), P())
    out_specs = (P("ctx", "head"), P(("ctx", "head"), None), P(("ctx", "head"), None))
    return jax.shard_map(local, mesh=mesh, in_specs=in_specs, out_specs=out_specs, check_vma=False)
```

time: 879 us -> 73.6 us (0.08)
  waiting for transfers between devices: 637 us -> 0 us
  matrix products: 100 us -> 0 us
  Pallas kernels: 0 us -> 67.6 us
  blocking collectives: 66.1 us -> 0 us
  local copies, waits for them, and re-layouts: 32.7 us -> 4.14 us
  other arithmetic: 15.1 us -> 0 us
  between operations: 13.9 us -> 0.66 us
  loops' own time: 12.4 us -> 0 us
    all_gather x2 -> x0, waiting for transfers between devices: 599 us -> none  [the longest x1 302 us: local(): lax.all_gather(value_rows, 'ctx', axis=0, tiled=True)]
    dot_general x112 -> x0, matrix products: 100 us -> none  [the longest x32 37.5 us: products(): jnp.einsum('qhd,kd->hqk', query_heads, key_block, preferred_element_type=...]
    pallas_call x0 -> x1, Pallas kernels: none -> 67.6 us  [local(): pl.pallas_call(kernel, out_shape=(jax.ShapeDtypeStruct((128, 256), BF16),...]
    all_to_all x1 -> x0, blocking collectives: 66.1 us -> none  [local(): lax.all_to_all(terms.astype(jnp.bfloat16), 'ctx', split_axis=0, concat_ax...]
    reduce_scatter x1 -> x0, waiting for transfers between devices: 35.8 us -> none  [local(): lax.psum_scatter(owned.astype(jnp.bfloat16), 'head', scatter_dimension=0,...]
    dynamic_slice x82 -> x0, local copies, waits for them, and re-layouts: 14.3 us -> none  [the longest x16 9.32 us: local(): lax.scan(backward, jnp.zeros((local_rows, local_heads, head_dim), jnp.flo...]
    dynamic_update_slice x32 -> x0, local copies, waits for them, and re-layouts: 13.8 us -> none  [local(): lax.scan(backward, jnp.zeros((local_rows, local_heads, head_dim), jnp.flo...]
    another operation x2 -> x0, loops' own time: 12.4 us -> none  [the longest x1 11.5 us: local(): lax.scan(backward, jnp.zeros((local_rows, local_heads, head_dim), jnp.flo...]
  transfers between devices with their start and end apart: 3 -> 0, of which waited for: 3 -> 0; matrix products, arithmetic and copies ran while one was open for 1% -> 0% of each run, Pallas kernels for 0% -> 0%
where the time goes in v1:
time: 73.6 us; the launch traced here: 72.4 us
  Pallas kernels  67.6 us (92%)
  local copies, waits for them, and re-layouts  4.14 us (6%)
    pallas_call x1, Pallas kernels, local(): pl.pallas_call(kernel, out_shape=(jax.ShapeDtypeStruct((128, 256), BF16),...  67.6 us
    unnamed x10, local copies, waits for them, and re-layouts  4.14 us

profile of v1, /device:TPU:6, one launch (start us, length us, event | category | flops | bytes accessed | tf_op | source)
XLA Modules:
  0.0 72.4 jit_solution(15688309595564235504)
XLA Ops:
  0.6 0.0 copy-start.2
  0.6 0.7 copy-done.2
  1.3 0.7 copy.9.order_ref
  2.0 67.6 %shard_map.85 = (bf16[128,256]{1,0:T(8,128)(2,1)}, bf16[16,128]{1,0:T(8,128)(2,1)}, bf16[16,128]{1,0:T(8,128)(2,1)}) custom-call(s32[8]{0:T(128)} %lens_ref.1, s32[64,2]{1,0:T(8,128)} %copy.9.order_ref, bf16[128,256]{1,0:T(8,128)(2,1)} %q_ref.1, bf16[128,256]{1,0:T(8,128)(2,1)} %g_ref.1, bf16[4,2,16,128]{3,2,1,0:T(8,128)(2,1)} %bitcast.2, ...), custom_call_target="tpu_custom_call" | custom-call | tf_op jit(solution)/shard_map/pallas_call | solution.py:386
  69.6 0.0 copy-start.1
  69.7 1.5 %copy.13 = bf16[128,256]{1,0:T(8,128)(2,1)} copy(bf16[128,256]{1,0:T(8,128)(2,1)} %get-tuple-element.6) | data formatting | bytes 131072
  71.1 0.0 copy-done.1
  71.1 0.0 copy-start
  71.1 0.6 copy.14
  71.7 0.1 copy-done
  71.8 0.6 copy.15
Async XLA Ops:
  0.6 0.7 copy-start.2
  69.6 1.5 %copy-start.1 = (bf16[16,128]{1,0:T(8,128)(2,1)S(1)}, bf16[16,128]{1,0:T(8,128)(2,1)}, u32[]{:S(2)}) copy-start(bf16[16,128]{1,0:T(8,128)(2,1)} %get-tuple-element.7) | copy-start | bytes 12292
  71.1 0.7 copy-start

commit v2 on v1

v2 whole, which is shorter than its diff:
```python
import functools
import math

import jax
import jax.numpy as jnp
from jax import lax
from jax.experimental import pallas as pl
from jax.experimental.pallas import tpu as pltpu
from jax.sharding import PartitionSpec as P

MESH = pl.DeviceIdType.MESH
F32 = jnp.float32
BF16 = jnp.bfloat16
NX, NY, NZH = 4, 8, 4
HD = 128
NEG = -1e30
SCALE = HD ** -0.5
EXP_SCALE = SCALE / math.log(2.0)
CK = 512
ROFF = (0, 1, 7, 2, 6, 3, 5, 4)
RPOS = {r: i for i, r in enumerate(ROFF)}
UQ = 256


def swap_rows(v, p):
    parts = [v[(k ^ p) * 2 : (k ^ p) * 2 + 2] for k in range(4)]
    return jnp.concatenate(parts, axis=0)


def kernel(
    lens_ref, order_ref, q_ref, g_ref, k_ref, v_ref,
    dq_ref, dk_ref, dv_ref,
    kv, qa, ga, qs, gs, kp, qlim, es, dps, ws, dss, dqa, pf, stm, st, rst, fac,
    dqb, dqr, sb, m1, rr, rl, yb, yr, zb, zr,
    lsem, qsend, qrecv, ysend, yrecv, xsend, xrecv, ssend, srecv, dsend, drecv,
    m1send, m1recv, rsend, rrecv, lsend, lrecv, rysend, ryrecv, zsend, zrecv,
    upsem, dnsem, nearsem,
):
    ctx = lax.axis_index("ctx")
    head = lax.axis_index("head")
    zl, y, x = ctx // 32, (ctx // 4) % 8, ctx % 4
    zh, core = head // 2, head % 2

    def at(zl_, y_, x_):
        return zl_ * 32 + y_ * 4 + x_

    right = (at(zl, y, (x + 1) % 4), head)
    left = (at(zl, y, (x + 3) % 4), head)
    ydev = [(at(zl, (y + r) % 8, x), head) for r in range(8)]
    zdev = [(ctx, ((zh + r) % 4) * 2 + core) for r in range(4)]
    gdev = [
        (at((zl + k // 2) % 2, y, x), zh * 2 + (core + k % 2) % 2) for k in range(4)
    ]
    zout = (at(1 - zl, y, x), ((zh + 3 + 2 * zl) % 4) * 2 + core)

    stage = [
        pltpu.make_async_copy(k_ref.at[:, core], kv.at[0, 0, 0], lsem.at[0]),
        pltpu.make_async_copy(v_ref.at[:, core], kv.at[1, 0, 0], lsem.at[1]),
        pltpu.make_async_copy(q_ref, qa.at[0], lsem.at[2]),
        pltpu.make_async_copy(g_ref, ga.at[0], lsem.at[3]),
    ]
    for c in stage:
        c.start()

    def signal(sem, dev):
        pl.semaphore_signal(sem, inc=1, device_id=dev, device_id_type=MESH)

    barrier = pltpu.get_barrier_semaphore()
    peers = [right, left, ydev[1], ydev[7], zout] + gdev[1:]
    for p in peers:
        signal(barrier, p)
    pl.semaphore_wait(barrier, len(peers))

    pending = []

    def send(src, dst, ss, rs, dev):
        c = pltpu.make_async_remote_copy(
            src_ref=src, dst_ref=dst, send_sem=ss, recv_sem=rs,
            device_id=dev, device_id_type=MESH,
        )
        c.start()
        pending.append(c)

    def landed(dst, ss, rs):
        pltpu.make_async_remote_copy(
            src_ref=dst, dst_ref=dst, send_sem=ss, recv_sem=rs,
            device_id=right, device_id_type=MESH,
        ).wait_recv()

    def blk(xr, r):
        return kv.at[:, RPOS[r % 8], xr]

    def x_forward(r):
        r = r % 8
        send(blk(0, r), blk(3, r), xsend.at[r, 0], xrecv.at[r, 0], right)
        send(blk(0, r), blk(1, r), xsend.at[r, 1], xrecv.at[r, 1], left)

    def y_send(r):
        r = r % 8
        send(blk(0, 0), blk(0, -r), ysend.at[r], yrecv.at[r], ydev[r])

    def y_landed(r):
        i = (-r) % 8
        landed(blk(0, r), ysend.at[i], yrecv.at[i])

    def x_arrive(r):
        r = r % 8
        landed(blk(3, r), xsend.at[r, 0], xrecv.at[r, 0])
        if r % 2 == 0:
            send(blk(3, r), blk(2, r), xsend.at[r, 2], xrecv.at[r, 2], right)
        landed(blk(1, r), xsend.at[r, 1], xrecv.at[r, 1])
        if r % 2 == 1:
            send(blk(1, r), blk(2, r), xsend.at[r, 2], xrecv.at[r, 2], left)

    def x_last(r):
        r = r % 8
        landed(blk(2, r), xsend.at[r, 2], xrecv.at[r, 2])

    signal(nearsem.at[0], zout)
    signal(nearsem.at[1], gdev[2])
    signal(upsem.at[0], ydev[1])
    signal(dnsem.at[0], ydev[7])
    stage[0].wait()
    stage[1].wait()
    y_send(1)
    y_send(7)
    x_forward(0)
    for k in (1, 2):
        send(q_ref, qa.at[k], qsend.at[k, 0], qrecv.at[k, 0], gdev[k])
        send(g_ref, ga.at[k], qsend.at[k, 1], qrecv.at[k, 1], gdev[k])
    pl.semaphore_wait(upsem.at[0], 1)
    signal(upsem.at[1], ydev[1])
    y_send(6)
    pl.semaphore_wait(dnsem.at[0], 1)
    signal(dnsem.at[1], ydev[7])
    y_send(2)
    pl.semaphore_wait(nearsem.at[0], 1)
    pl.semaphore_wait(nearsem.at[1], 1)
    signal(nearsem.at[2], zdev[3])
    pl.semaphore_wait(upsem.at[1], 1)
    signal(upsem.at[2], ydev[1])
    y_send(5)
    pl.semaphore_wait(dnsem.at[1], 1)
    y_send(3)
    pl.semaphore_wait(upsem.at[2], 1)
    y_send(4)

    lane = lax.broadcasted_iota(jnp.int32, (8, HD), 1) % 64
    starts = []
    total = jnp.int32(0)
    for i in range(8):
        starts.append(total)
        total = total + lens_ref[i]
    for dz in range(2):
        octx = at((zl + dz) % 2, y, x)
        for h in range(2):
            u = dz * 2 + h
            qp = order_ref[h, octx] * 64 + lane
            first = jnp.zeros_like(qp)
            for s in starts:
                first = jnp.maximum(first, jnp.where(qp >= s, s, 0))
            qlim[u, 0] = qp
            qlim[u, 1] = first
    row = lax.broadcasted_iota(jnp.int32, (32, HD), 0)
    pattern = (row // 16) * 32 + row % 16 + core * 16
    for rp in range(8):
        for xr in range(4):
            octx = at(zl, (y + ROFF[rp]) % 8, (x + xr) % 4)
            for h in range(2):
                o = ((rp % 2) * 4 + xr) * 64 + h * 32
                kp[rp // 2, o : o + 32, :] = pattern + order_ref[h, octx] * 64

    def units(dz):
        for h in range(2):
            u = dz * 2 + h
            for dc in range(2):
                for hd in range(2):
                    rows = slice(h * 64, h * 64 + 64)
                    cols = slice(hd * HD, hd * HD + HD)
                    o = (dc * 2 + hd) * 64
                    qs[u, o : o + 64, :] = qa[dz * 2 + dc, rows, cols]
                    gs[u, o : o + 64, :] = ga[dz * 2 + dc, rows, cols]

    def pass1(j, dz):
        keys = kv[0, 2 * j : 2 * j + 2].reshape(CK, HD)
        vals = kv[1, 2 * j : 2 * j + 2].reshape(CK, HD)
        dims = (((1,), (1,)), ((), ()))
        for h in range(2):
            u = dz * 2 + h
            s = lax.dot_general(keys, qs[u], dims, preferred_element_type=F32)
            dp = lax.dot_general(vals, gs[u], dims, preferred_element_type=F32)
            dps[j, u] = dp
            pos = kp[j]
            allowed = (pos <= qlim[u, 0, 0:1, :]) & (pos >= qlim[u, 1, 0:1, :])
            for dc in range(2):
                cols = slice(dc * HD, dc * HD + HD)
                row = (dz * 2 + dc) * 2 + h
                sh = jnp.where(allowed, s[:, cols], NEG)
                m = jnp.max(sh, axis=0, keepdims=True)
                e = jnp.exp2((sh - m) * EXP_SCALE)
                es[j, u, :, cols] = e
                stm[j, 0, row : row + 1, :] = m
                stm[j, 1, row : row + 1, :] = jnp.sum(e, axis=0, keepdims=True)
                stm[j, 2, row : row + 1, :] = jnp.sum(e * dp[:, cols], axis=0, keepdims=True)

    def q_landed(k):
        landed(qa.at[k], qsend.at[k, 0], qrecv.at[k, 0])
        landed(ga.at[k], qsend.at[k, 1], qrecv.at[k, 1])

    y_landed(1)
    x_forward(1)
    y_landed(7)
    x_forward(7)
    x_arrive(0)
    stage[2].wait()
    stage[3].wait()
    q_landed(1)
    units(0)
    y_landed(2)
    x_forward(2)
    y_landed(6)
    x_forward(6)
    q_landed(2)
    send(qa.at[2], qa.at[3], qsend.at[3, 0], qrecv.at[3, 0], gdev[1])
    send(ga.at[2], ga.at[3], qsend.at[3, 1], qrecv.at[3, 1], gdev[1])
    x_arrive(1)
    x_arrive(7)
    y_landed(3)
    x_forward(3)
    y_landed(5)
    x_forward(5)
    x_last(0)
    x_last(1)
    pass1(0, 0)
    y_landed(4)
    x_forward(4)
    x_arrive(2)
    x_arrive(6)
    q_landed(3)
    units(1)
    pass1(0, 1)
    x_arrive(3)
    x_arrive(5)
    x_last(7)
    x_last(2)
    pass1(1, 0)
    x_arrive(4)
    pass1(1, 1)
    x_last(6)
    x_last(3)
    pass1(2, 0)
    pass1(2, 1)
    x_last(5)
    x_last(4)
    pass1(3, 0)
    pass1(3, 1)
    pl.semaphore_wait(nearsem.at[2], 1)

    def top(vals):
        return jnp.maximum(jnp.maximum(vals[0], vals[1]), jnp.maximum(vals[2], vals[3]))

    ms = [stm[j, 0] for j in range(4)]
    m = top(ms)
    sc = [jnp.exp2((a - m) * EXP_SCALE) for a in ms]
    st[0] = m
    st[1] = sum(sc[j] * stm[j, 1] for j in range(4))
    st[2] = sum(sc[j] * stm[j, 2] for j in range(4))
    for k in range(1, 4):
        send(st, rst.at[k], ssend.at[k], srecv.at[k], gdev[k])
    for k in range(1, 4):
        landed(rst.at[k], ssend.at[k], srecv.at[k])
    got = [[st[i]] + [swap_rows(rst[p, i], p) for p in range(1, 4)] for i in range(3)]
    gm = top(got[0])
    sc = [jnp.exp2((a - gm) * EXP_SCALE) for a in got[0]]
    inv = 1.0 / sum(sc[p] * got[1][p] for p in range(4))
    fac[4] = sum(sc[p] * got[2][p] for p in range(4)) * inv
    for j in range(4):
        fac[j] = jnp.exp2((ms[j] - gm) * EXP_SCALE) * inv

    def column(c, first):
        for u in range(4):
            dz, h = u // 2, u % 2
            for dc in range(2):
                row = (dz * 2 + dc) * 2 + h
                cols = slice(dc * HD, dc * HD + HD)
                o = u * UQ + dc * HD
                delta = fac[4, row : row + 1, :]
                for rp in range(8):
                    j = rp // 2
                    ko = ((rp % 2) * 4 + c) * 64
                    w = es[j, u, ko : ko + 64, cols] * fac[j, row : row + 1, :]
                    ws[rp * 64 : rp * 64 + 64, o : o + HD] = w.astype(BF16)
                    d = w * (dps[j, u, ko : ko + 64, cols] - delta)
                    dss[rp * 64 : rp * 64 + 64, o : o + HD] = d.astype(BF16)
        dims = (((1,), (0,)), ((), ()))
        q_all = qs[...].reshape(4 * UQ, HD)
        g_all = gs[...].reshape(4 * UQ, HD)
        dkc = lax.dot_general(dss[...], q_all, dims, preferred_element_type=F32)
        pf[c, 0] = dkc.reshape(8, 64, HD)
        dvc = lax.dot_general(ws[...], g_all, dims, preferred_element_type=F32)
        pf[c, 1] = dvc.reshape(8, 64, HD)
        keys = kv[0, :, c].reshape(CK, HD)
        part = lax.dot_general(
            dss[...], keys, (((0,), (0,)), ((), ())), preferred_element_type=F32
        )
        if first:
            dqa[...] = part
        else:
            dqa[...] += part

    def mine(c, r):
        return pf[c, :, RPOS[r]]

    order = [4, 3, 5, 2, 6, 1, 7, 0]
    column(2, True)
    for r in order:
        sb[2, r] = mine(2, r).astype(BF16)
        dev = right if r % 2 == 0 else left
        send(sb.at[2, r], m1.at[r], m1send.at[r], m1recv.at[r], dev)
    column(1, False)
    for r in order:
        if r % 2 == 1:
            sb[1, r] = mine(1, r).astype(BF16)
            send(sb.at[1, r], rr.at[r], rsend.at[r], rrecv.at[r], right)
    column(3, False)
    for r in order:
        if r % 2 == 0:
            sb[3, r] = mine(3, r).astype(BF16)
            send(sb.at[3, r], rl.at[r], lsend.at[r], lrecv.at[r], left)
    for r in order:
        landed(m1.at[r], m1send.at[r], m1recv.at[r])
        c = 1 if r % 2 == 0 else 3
        sb[c, r] = (mine(c, r) + m1[r].astype(F32)).astype(BF16)
        if r % 2 == 0:
            send(sb.at[1, r], rr.at[r], rsend.at[r], rrecv.at[r], right)
        else:
            send(sb.at[3, r], rl.at[r], lsend.at[r], lrecv.at[r], left)
    column(0, False)

    for k in range(4):
        dz, dc = k // 2, k % 2
        for h in range(2):
            for hd in range(2):
                o = (dz * 2 + h) * UQ + (dc * 2 + hd) * 64
                rows = slice(h * 64, h * 64 + 64)
                cols = slice(hd * HD, hd * HD + HD)
                part = dqa[o : o + 64, :]
                if k == 0:
                    dq_ref[rows, cols] = part.astype(BF16)
                else:
                    dqb[k, rows, cols] = part.astype(BF16)
        if k > 0:
            send(dqb.at[k], dqr.at[k], dsend.at[k], drecv.at[k], gdev[k])

    own = None
    for r in order:
        landed(rr.at[r], rsend.at[r], rrecv.at[r])
        landed(rl.at[r], lsend.at[r], lrecv.at[r])
        t = mine(0, r) + rr[r].astype(F32) + rl[r].astype(F32)
        if r == 0:
            own = t
        else:
            yb[r] = t.astype(BF16)
            send(yb.at[r], yr.at[r], rysend.at[r], ryrecv.at[r], ydev[r])
    for k in range(1, 4):
        landed(dqr.at[k], dsend.at[k], drecv.at[k])
    for h in range(2):
        for hd in range(2):
            o = h * UQ + hd * 64
            rows = slice(h * 64, h * 64 + 64)
            cols = slice(hd * HD, hd * HD + HD)
            t = dqa[o : o + 64, :]
            for k in range(1, 4):
                t = t + dqr[k, rows, cols].astype(F32)
            dq_ref[rows, cols] = (t * SCALE).astype(BF16)
    for r in (1, 7, 2, 6, 3, 5, 4):
        landed(yr.at[r], rysend.at[r], ryrecv.at[r])
        own = own + yr[r].astype(F32)
    pf[0, :, 0] = own
    for r in range(1, 4):
        o = pl.multiple_of(((zh + r) % 4) * 16, 16)
        zb[r] = pf[0, :, 0, pl.ds(o, 16), :].astype(BF16)
        send(zb.at[r], zr.at[r], zsend.at[r], zrecv.at[r], zdev[r])
    fin = pf[0, :, 0, pl.ds(pl.multiple_of(zh * 16, 16), 16), :]
    for r in range(1, 4):
        landed(zr.at[r], zsend.at[r], zrecv.at[r])
        fin = fin + zr[r].astype(F32)
    dk_ref[...] = (fin[0] * SCALE).astype(BF16)
    dv_ref[...] = fin[1].astype(BF16)
    for c in pending:
        c.wait_send()


def local(queries, key_rows, value_rows, out_grad, doc_lengths, span_order):
    vm = pltpu.VMEM
    dma = pltpu.SemaphoreType.DMA
    piece = (2, 64, HD)
    scratch = [
        vm((2, NY, NX, 4, 16, HD), BF16),
        vm((4, 128, 256), BF16),
        vm((4, 128, 256), BF16),
        vm((4, UQ, HD), BF16),
        vm((4, UQ, HD), BF16),
        vm((NX, CK, HD), jnp.int32),
        vm((4, 2, 8, HD), jnp.int32),
        vm((NX, 4, CK, UQ), F32),
        vm((NX, 4, CK, UQ), F32),
        vm((CK, 4 * UQ), BF16),
        vm((CK, 4 * UQ), BF16),
        vm((4 * UQ, HD), F32),
        vm((4, 2, 8, 64, HD), F32),
        vm((4, 3, 8, HD), F32),
        vm((3, 8, HD), F32),
        vm((4, 3, 8, HD), F32),
        vm((5, 8, HD), F32),
        vm((4, 128, 256), BF16),
        vm((4, 128, 256), BF16),
        vm((4, 8) + piece, BF16),
        vm((8,) + piece, BF16),
        vm((8,) + piece, BF16),
        vm((8,) + piece, BF16),
        vm((8,) + piece, BF16),
        vm((8,) + piece, BF16),
        vm((4, 2, 16, HD), BF16),
        vm((4, 2, 16, HD), BF16),
        dma((4,)),
        dma((4, 2)), dma((4, 2)),
        dma((8,)), dma((8,)),
        dma((8, 3)), dma((8, 3)),
        dma((4,)), dma((4,)),
        dma((4,)), dma((4,)),
        dma((8,)), dma((8,)),
        dma((8,)), dma((8,)),
        dma((8,)), dma((8,)),
        dma((8,)), dma((8,)),
        dma((4,)), dma((4,)),
        pltpu.SemaphoreType.REGULAR((3,)),
        pltpu.SemaphoreType.REGULAR((2,)),
        pltpu.SemaphoreType.REGULAR((3,)),
    ]
    smem = pl.BlockSpec(memory_space=pltpu.SMEM)
    hbm = pl.BlockSpec(memory_space=pl.ANY)
    vmem = pl.BlockSpec(memory_space=pltpu.VMEM)
    return pl.pallas_call(
        kernel,
        out_shape=(
            vm((128, 256), BF16),
            vm((16, HD), BF16),
            vm((16, HD), BF16),
        ),
        in_specs=[smem, smem, hbm, hbm, hbm, hbm],
        out_specs=(vmem, vmem, vmem),
        scratch_shapes=scratch,
        compiler_params=pltpu.CompilerParams(
            collective_id=0, has_side_effects=True, vmem_limit_bytes=60 * 1024 * 1024
        ),
    )(
        doc_lengths,
        span_order.T,
        queries,
        out_grad,
        key_rows.reshape(4, 2, 16, HD),
        value_rows.reshape(4, 2, 16, HD),
    )


def solution(mesh):
    in_specs = (P("ctx", "head"), P("ctx", None), P("ctx", None), P("ctx", "head"), P(), P())
    out_specs = (P("ctx", "head"), P(("ctx", "head"), None), P(("ctx", "head"), None))
    return jax.shard_map(local, mesh=mesh, in_specs=in_specs, out_specs=out_specs, check_vma=False)
```

time: 73.6 us -> 61.7 us (0.84)
  Pallas kernels: 67.6 us -> 58.5 us
  local copies, waits for them, and re-layouts: 4.14 us -> 1.82 us
    pallas_call x1, Pallas kernels: 67.6 us -> 58.5 us  [local(): pl.pallas_call(kernel, out_shape=(vm((128, 256), BF16), vm((16, HD), BF16...]
    unnamed x10 -> x3, local copies, waits for them, and re-layouts: 4.14 us -> 1.82 us
where the time goes in v2:
time: 61.7 us; the launch traced here: 61 us
  Pallas kernels  58.5 us (95%)
  local copies, waits for them, and re-layouts  1.82 us (3%)
  between operations  0.64 us (1%)
    pallas_call x1, Pallas kernels, local(): pl.pallas_call(kernel, out_shape=(vm((128, 256), BF16), vm((16, HD), BF16...  58.5 us
    unnamed x3, local copies, waits for them, and re-layouts  1.82 us

profile of v2, /device:TPU:6, one launch (start us, length us, event | category | flops | bytes accessed | tf_op | source)
XLA Modules:
  0.0 61.0 jit_solution(14713254695586539953)
XLA Ops:
  0.6 58.5 %shard_map.85 = (bf16[128,256]{1,0:T(8,128)(2,1)S(1)}, bf16[16,128]{1,0:T(8,128)(2,1)S(1)}, bf16[16,128]{1,0:T(8,128)(2,1)S(1)}) custom-call(s32[8]{0:T(128)} %lens_ref.1, s32[2,64]{1,0:T(2,128)} %bitcast.5, bf16[128,256]{1,0:T(8,128)(2,1)} %q_ref.1, bf16[128,256]{1,0:T(8,128)(2,1)} %g_ref.1, bf16[4,2,16,128]{3,2,1,0:T(8,128)(2,1)} %bitcast.3, ...), custom_call_target="tpu_custom_call" | custom-call | tf_op jit(solution)/shard_map/pallas_call | solution.py:444
  59.2 0.6 %copy.12 = bf16[128,256]{1,0:T(8,128)(2,1)} copy(bf16[128,256]{1,0:T(8,128)(2,1)S(1)} %get-tuple-element.3) | data formatting | bytes 131072
  59.8 0.6 copy.13
  60.4 0.6 copy.14

commit v3 on v2

v3 whole, which is shorter than its diff:
```python
import functools
import math

import jax
import jax.numpy as jnp
from jax import lax
from jax.experimental import pallas as pl
from jax.experimental.pallas import tpu as pltpu
from jax.sharding import PartitionSpec as P

MESH = pl.DeviceIdType.MESH
F32 = jnp.float32
BF16 = jnp.bfloat16
NU = 8
HD = 128
NEG = -1e30
SCALE = HD ** -0.5
EXP_SCALE = SCALE / math.log(2.0)
CK = 256
ROFF = (0, 1, 7, 2, 6, 3, 5, 4)
RPOS = {r: i for i, r in enumerate(ROFF)}
UQ = 256


def swap_rows(v, p):
    parts = [v[(k ^ p) * 2 : (k ^ p) * 2 + 2] for k in range(4)]
    return jnp.concatenate(parts, axis=0)


def kernel(
    lens_ref, order_ref, q_ref, g_ref, k_ref, v_ref,
    dq_ref, dk_ref, dv_ref,
    kv, qa, ga, qs, gs, kp, qlim, es, dps, ws, dss, dqa, pf, stm, st, rst, fac,
    dqb, dqr, sb, xr, yb, yr, zb, zr,
    lsem, qsend, qrecv, ysend, yrecv, xsend, xrecv, ssend, srecv, dsend, drecv,
    rsend, rrecv, rysend, ryrecv, zsend, zrecv, nearsem,
):
    ctx = lax.axis_index("ctx")
    head = lax.axis_index("head")
    zl, y, x = ctx // 32, (ctx // 4) % 8, ctx % 4
    zh, core = head // 2, head % 2
    xg = x + 1 - 2 * (x % 2)
    xo = (x + 3 + 2 * (x % 2)) % 4

    def at(zl_, y_, x_):
        return zl_ * 32 + y_ * 4 + x_

    odev = (at(zl, y, xo), head)
    ydev = [(at(zl, (y + r) % 8, x), head) for r in range(8)]
    zdev = [(ctx, ((zh + r) % 4) * 2 + core) for r in range(4)]
    gdev = [
        (
            at((zl + (k // 2) % 2) % 2, y, xg if k // 4 else x),
            zh * 2 + (core + k % 2) % 2,
        )
        for k in range(8)
    ]
    zout = (at(1 - zl, y, x), ((zh + 3 + 2 * zl) % 4) * 2 + core)

    stage = [
        pltpu.make_async_copy(k_ref.at[:, core], kv.at[0, 0, 0], lsem.at[0]),
        pltpu.make_async_copy(v_ref.at[:, core], kv.at[1, 0, 0], lsem.at[1]),
        pltpu.make_async_copy(q_ref, qa.at[0], lsem.at[2]),
        pltpu.make_async_copy(g_ref, ga.at[0], lsem.at[3]),
    ]
    for c in stage:
        c.start()

    def signal(sem, dev):
        pl.semaphore_signal(sem, inc=1, device_id=dev, device_id_type=MESH)

    barrier = pltpu.get_barrier_semaphore()
    peers = [odev, ydev[1], ydev[7], ydev[2], ydev[6], zout] + gdev[1:]
    for p in peers:
        signal(barrier, p)
    pl.semaphore_wait(barrier, len(peers))

    pending = []

    def send(src, dst, ss, rs, dev):
        c = pltpu.make_async_remote_copy(
            src_ref=src, dst_ref=dst, send_sem=ss, recv_sem=rs,
            device_id=dev, device_id_type=MESH,
        )
        c.start()
        pending.append(c)

    def landed(dst, ss, rs):
        pltpu.make_async_remote_copy(
            src_ref=dst, dst_ref=dst, send_sem=ss, recv_sem=rs,
            device_id=odev, device_id_type=MESH,
        ).wait_recv()

    def blk(i, c, r):
        return kv.at[i, RPOS[r % 8], c]

    def x_forward(r):
        r = r % 8
        for i in range(2):
            send(blk(i, 0, r), blk(i, 1, r), xsend.at[r, i], xrecv.at[r, i], odev)

    def x_landed(r):
        r = r % 8
        for i in range(2):
            landed(blk(i, 1, r), xsend.at[r, i], xrecv.at[r, i])

    def y_send(i, src, dst, to, sem):
        send(blk(i, 0, src), blk(i, 0, dst), ysend.at[sem, i], yrecv.at[sem, i], ydev[to])

    def y_landed(i, r, sem):
        landed(blk(i, 0, r), ysend.at[sem, i], yrecv.at[sem, i])

    stage[0].wait()
    y_send(0, 0, 6, 2, 2)
    y_send(0, 0, 2, 6, 6)
    stage[1].wait()
    y_send(1, 0, 6, 2, 2)
    y_send(1, 0, 2, 6, 6)
    x_forward(0)
    for i in range(2):
        y_send(i, 0, 7, 1, 1)
        y_send(i, 0, 1, 7, 7)
    for k in (2, 4, 1):
        send(q_ref, qa.at[k], qsend.at[k, 0], qrecv.at[k, 0], gdev[k])
        send(g_ref, ga.at[k], qsend.at[k, 1], qrecv.at[k, 1], gdev[k])
    signal(nearsem.at[0], zout)
    signal(nearsem.at[1], gdev[2])

    lane = lax.broadcasted_iota(jnp.int32, (8, HD), 1) % 64
    starts = []
    total = jnp.int32(0)
    for i in range(8):
        starts.append(total)
        total = total + lens_ref[i]
    for g in range(4):
        octx = at((zl + g % 2) % 2, y, xg if g // 2 else x)
        for h in range(2):
            u = g * 2 + h
            qp = order_ref[h, octx] * 64 + lane
            first = jnp.zeros_like(qp)
            for s in starts:
                first = jnp.maximum(first, jnp.where(qp >= s, s, 0))
            qlim[u, 0] = qp
            qlim[u, 1] = first
    row = lax.broadcasted_iota(jnp.int32, (32, HD), 0)
    pattern = (row // 16) * 32 + row % 16 + core * 16
    for rp in range(8):
        for c in range(2):
            octx = at(zl, (y + ROFF[rp]) % 8, xo if c else x)
            for h in range(2):
                o = ((rp % 2) * 2 + c) * 64 + h * 32
                kp[rp // 2, o : o + 32, :] = pattern + order_ref[h, octx] * 64

    def units(g):
        for h in range(2):
            u = g * 2 + h
            for dc in range(2):
                for hd in range(2):
                    rows = slice(h * 64, h * 64 + 64)
                    cols = slice(hd * HD, hd * HD + HD)
                    o = (dc * 2 + hd) * 64
                    qs[u, o : o + 64, :] = qa[g * 2 + dc, rows, cols]
                    gs[u, o : o + 64, :] = ga[g * 2 + dc, rows, cols]

    def pass1(j, g):
        keys = kv[0, 2 * j : 2 * j + 2].reshape(CK, HD)
        vals = kv[1, 2 * j : 2 * j + 2].reshape(CK, HD)
        dims = (((1,), (1,)), ((), ()))
        for h in range(2):
            u = g * 2 + h
            s = lax.dot_general(keys, qs[u], dims, preferred_element_type=F32)
            dp = lax.dot_general(vals, gs[u], dims, preferred_element_type=F32)
            dps[j, u] = dp
            pos = kp[j]
            allowed = (pos <= qlim[u, 0, 0:1, :]) & (pos >= qlim[u, 1, 0:1, :])
            for dc in range(2):
                cols = slice(dc * HD, dc * HD + HD)
                row = (g * 2 + dc) * 2 + h
                sh = jnp.where(allowed, s[:, cols], NEG)
                m = jnp.max(sh, axis=0, keepdims=True)
                e = jnp.exp2((sh - m) * EXP_SCALE)
                es[j, u, :, cols] = e
                stm[j, 0, row : row + 1, :] = m
                stm[j, 1, row : row + 1, :] = jnp.sum(e, axis=0, keepdims=True)
                stm[j, 2, row : row + 1, :] = jnp.sum(e * dp[:, cols], axis=0, keepdims=True)

    def q_landed(k):
        landed(qa.at[k], qsend.at[k, 0], qrecv.at[k, 0])

    def g_landed(k):
        landed(ga.at[k], qsend.at[k, 1], qrecv.at[k, 1])

    def q_pass(k, to, dev):
        send(qa.at[k], qa.at[to], qsend.at[to, 0], qrecv.at[to, 0], dev)

    def g_pass(k, to, dev):
        send(ga.at[k], ga.at[to], qsend.at[to, 1], qrecv.at[to, 1], dev)

    stage[2].wait()
    stage[3].wait()
    q_landed(1)
    g_landed(1)
    units(0)
    for i in range(2):
        y_landed(i, 6, 2)
        y_send(i, 6, 5, 1, 3)
        if i == 0:
            y_send(0, 6, 4, 2, 4)
        y_landed(i, 2, 6)
        y_send(i, 2, 3, 7, 5)
        if i == 1:
            y_send(1, 2, 4, 6, 4)
    for i in range(2):
        y_landed(i, 7, 1)
        y_landed(i, 1, 7)
    x_forward(7)
    x_forward(1)
    x_forward(2)
    x_forward(6)
    q_landed(2)
    q_pass(2, 6, gdev[4])
    q_pass(2, 3, gdev[1])
    q_landed(4)
    q_pass(4, 5, gdev[1])
    g_landed(4)
    g_pass(4, 6, gdev[2])
    g_pass(4, 5, gdev[1])
    g_landed(2)
    g_pass(2, 3, gdev[1])
    x_landed(0)
    x_landed(1)
    pl.semaphore_wait(nearsem.at[0], 1)
    pl.semaphore_wait(nearsem.at[1], 1)
    signal(nearsem.at[2], zdev[3])
    pass1(0, 0)
    for i in range(2):
        y_landed(i, 5, 3)
    x_forward(5)
    for i in range(2):
        y_landed(i, 3, 5)
    x_forward(3)
    y_landed(0, 4, 4)
    y_landed(1, 4, 4)
    x_forward(4)
    q_landed(6)
    q_pass(6, 7, gdev[1])
    g_landed(6)
    g_pass(6, 7, gdev[1])
    q_landed(3)
    g_landed(3)
    units(1)
    pass1(0, 1)
    q_landed(5)
    g_landed(5)
    units(2)
    pass1(0, 2)
    x_landed(7)
    x_landed(2)
    pass1(1, 0)
    pass1(1, 1)
    pass1(1, 2)
    q_landed(7)
    g_landed(7)
    units(3)
    pass1(0, 3)
    pass1(1, 3)
    x_landed(6)
    x_landed(3)
    for g in range(4):
        pass1(2, g)
    x_landed(5)
    x_landed(4)
    def top(vals):
        while len(vals) > 1:
            vals = [jnp.maximum(a, b) for a, b in zip(vals[::2], vals[1::2])]
        return vals[0]

    def own_stats(dx):
        rows = slice(dx * 8, dx * 8 + 8)
        ms = [stm[j, 0, rows] for j in range(4)]
        m = top(ms)
        sc = [jnp.exp2((a - m) * EXP_SCALE) for a in ms]
        st[dx, 0] = m
        st[dx, 1] = sum(sc[j] * stm[j, 1, rows] for j in range(4))
        st[dx, 2] = sum(sc[j] * stm[j, 2, rows] for j in range(4))
        for k in (6, 7, 4, 5, 2, 3, 1):
            to = rst.at[k, (dx + k // 4) % 2]
            send(st.at[dx], to, ssend.at[k, dx], srecv.at[k, (dx + k // 4) % 2], gdev[k])

    pass1(3, 0)
    pass1(3, 1)
    own_stats(0)
    pass1(3, 2)
    pass1(3, 3)
    own_stats(1)
    pl.semaphore_wait(nearsem.at[2], 1)
    for dx in range(2):
        rows = slice(dx * 8, dx * 8 + 8)
        for k in range(1, 8):
            landed(rst.at[k, dx], ssend.at[k, dx], srecv.at[k, dx])
        got = [[st[dx, i]] + [swap_rows(rst[p, dx, i], p % 4) for p in range(1, 8)] for i in range(3)]
        gm = top(got[0])
        sc = [jnp.exp2((a - gm) * EXP_SCALE) for a in got[0]]
        inv = 1.0 / sum(sc[p] * got[1][p] for p in range(8))
        fac[4, rows] = sum(sc[p] * got[2][p] for p in range(8)) * inv
        for j in range(4):
            fac[j, rows] = jnp.exp2((stm[j, 0, rows] - gm) * EXP_SCALE) * inv

    def block(c, j0, nj, first):
        nk = nj * 128
        for u in range(NU):
            g, h = u // 2, u % 2
            for dc in range(2):
                row = (g * 2 + dc) * 2 + h
                cols = slice(dc * HD, dc * HD + HD)
                o = u * UQ + dc * HD
                delta = fac[4, row : row + 1, :]
                for i in range(2 * nj):
                    j = j0 + i // 2
                    ko = ((i % 2) * 2 + c) * 64
                    w = es[j, u, ko : ko + 64, cols] * fac[j, row : row + 1, :]
                    ws[i * 64 : i * 64 + 64, o : o + HD] = w.astype(BF16)
                    d = w * (dps[j, u, ko : ko + 64, cols] - delta)
                    dss[i * 64 : i * 64 + 64, o : o + HD] = d.astype(BF16)
        dims = (((1,), (0,)), ((), ()))
        q_all = qs[...].reshape(NU * UQ, HD)
        g_all = gs[...].reshape(NU * UQ, HD)
        r0, n = 2 * j0, 2 * nj
        dkc = lax.dot_general(dss[0:nk], q_all, dims, preferred_element_type=F32)
        pf[c, 0, r0 : r0 + n] = dkc.reshape(n, 64, HD)
        dvc = lax.dot_general(ws[0:nk], g_all, dims, preferred_element_type=F32)
        pf[c, 1, r0 : r0 + n] = dvc.reshape(n, 64, HD)
        keys = kv[0, r0 : r0 + n, c].reshape(nk, HD)
        add = lax.dot_general(
            dss[0:nk], keys, (((0,), (0,)), ((), ())), preferred_element_type=F32
        )
        if first:
            dqa[...] = add
        else:
            dqa[...] += add

    def mine(c, r):
        return pf[c, :, RPOS[r]]

    def x_send(r):
        sb[r] = mine(1, r).astype(BF16)
        send(sb.at[r], xr.at[r], rsend.at[r], rrecv.at[r], odev)

    def column_sum(r):
        landed(xr.at[r], rsend.at[r], rrecv.at[r])
        return mine(0, r) + xr[r].astype(F32)

    def y_out(r, to):
        send(yb.at[r], yr.at[r], rysend.at[r], ryrecv.at[r], ydev[to])

    def y_in(r):
        landed(yr.at[r], rysend.at[r], ryrecv.at[r])

    block(1, 3, 1, True)
    x_send(4)
    x_send(5)
    block(1, 2, 1, False)
    x_send(3)
    x_send(6)
    block(0, 2, 2, False)
    block(1, 0, 2, False)
    for r in (2, 1, 7, 0):
        x_send(r)
    yb[4] = column_sum(4).astype(BF16)
    send(yb.at[4, 0], yr.at[4, 0], rysend.at[4], ryrecv.at[4], ydev[2])
    send(yb.at[4, 1], yr.at[4, 1], rysend.at[0], ryrecv.at[0], ydev[6])
    block(0, 0, 2, False)
    yb[5] = column_sum(5).astype(BF16)
    y_out(5, 7)
    yb[3] = column_sum(3).astype(BF16)
    y_out(3, 1)

    def dq_part(k, h, hd):
        o = ((k // 2) * 2 + h) * UQ + ((k % 2) * 2 + hd) * 64
        return dqa[o : o + 64, :]

    for k in (6, 7, 4, 5, 2, 3, 1):
        for h in range(2):
            for hd in range(2):
                rows = slice(h * 64, h * 64 + 64)
                cols = slice(hd * HD, hd * HD + HD)
                dqb[k, rows, cols] = dq_part(k, h, hd).astype(BF16)
        send(dqb.at[k], dqr.at[k], dsend.at[k], drecv.at[k], gdev[k])

    t6 = column_sum(6)
    t2 = column_sum(2)
    y_in(5)
    landed(yr.at[4, 1], rysend.at[0], ryrecv.at[0])
    yb[6, 0] = (t6[0] + yr[5, 0].astype(F32)).astype(BF16)
    yb[6, 1] = (t6[1] + yr[5, 1].astype(F32) + yr[4, 1].astype(F32)).astype(BF16)
    y_out(6, 6)
    y_in(3)
    landed(yr.at[4, 0], rysend.at[4], ryrecv.at[4])
    yb[2, 0] = (t2[0] + yr[3, 0].astype(F32) + yr[4, 0].astype(F32)).astype(BF16)
    yb[2, 1] = (t2[1] + yr[3, 1].astype(F32)).astype(BF16)
    y_out(2, 2)
    yb[1] = column_sum(1).astype(BF16)
    y_out(1, 1)
    yb[7] = column_sum(7).astype(BF16)
    y_out(7, 7)
    own = column_sum(0)
    for r in (1, 7, 2, 6):
        y_in(r)
        own = own + yr[r].astype(F32)
    pf[0, :, 0] = own
    for r in (2, 1, 3):
        o = pl.multiple_of(((zh + r) % 4) * 16, 16)
        zb[r] = pf[0, :, 0, pl.ds(o, 16), :].astype(BF16)
        send(zb.at[r], zr.at[r], zsend.at[r], zrecv.at[r], zdev[r])
    fin = pf[0, :, 0, pl.ds(pl.multiple_of(zh * 16, 16), 16), :]
    for k in range(1, 8):
        landed(dqr.at[k], dsend.at[k], drecv.at[k])
    for h in range(2):
        for hd in range(2):
            rows = slice(h * 64, h * 64 + 64)
            cols = slice(hd * HD, hd * HD + HD)
            t = dq_part(0, h, hd)
            for k in range(1, 8):
                t = t + dqr[k, rows, cols].astype(F32)
            dq_ref[rows, cols] = (t * SCALE).astype(BF16)
    for c in pending:
        c.wait_send()
    for r in (1, 3, 2):
        landed(zr.at[r], zsend.at[r], zrecv.at[r])
        fin = fin + zr[r].astype(F32)
    dk_ref[...] = (fin[0] * SCALE).astype(BF16)
    dv_ref[...] = fin[1].astype(BF16)


def local(queries, key_rows, value_rows, out_grad, doc_lengths, span_order):
    vm = pltpu.VMEM
    dma = pltpu.SemaphoreType.DMA
    piece = (2, 64, HD)
    scratch = [
        vm((2, 8, 2, 4, 16, HD), BF16),
        vm((8, 128, 256), BF16),
        vm((8, 128, 256), BF16),
        vm((NU, UQ, HD), BF16),
        vm((NU, UQ, HD), BF16),
        vm((4, CK, HD), jnp.int32),
        vm((NU, 2, 8, HD), jnp.int32),
        vm((4, NU, CK, UQ), F32),
        vm((4, NU, CK, UQ), F32),
        vm((CK, NU * UQ), BF16),
        vm((CK, NU * UQ), BF16),
        vm((NU * UQ, HD), F32),
        vm((2, 2, 8, 64, HD), F32),
        vm((4, 3, 16, HD), F32),
        vm((2, 3, 8, HD), F32),
        vm((8, 2, 3, 8, HD), F32),
        vm((5, 16, HD), F32),
        vm((8, 128, 256), BF16),
        vm((8, 128, 256), BF16),
        vm((8,) + piece, BF16),
        vm((8,) + piece, BF16),
        vm((8,) + piece, BF16),
        vm((8,) + piece, BF16),
        vm((4, 2, 16, HD), BF16),
        vm((4, 2, 16, HD), BF16),
        dma((4,)),
        dma((8, 2)), dma((8, 2)),
        dma((8, 2)), dma((8, 2)),
        dma((8, 2)), dma((8, 2)),
        dma((8, 2)), dma((8, 2)),
        dma((8,)), dma((8,)),
        dma((8,)), dma((8,)),
        dma((8,)), dma((8,)),
        dma((4,)), dma((4,)),
        pltpu.SemaphoreType.REGULAR((3,)),
    ]
    smem = pl.BlockSpec(memory_space=pltpu.SMEM)
    hbm = pl.BlockSpec(memory_space=pl.ANY)
    vmem = pl.BlockSpec(memory_space=pltpu.VMEM)
    return pl.pallas_call(
        kernel,
        out_shape=(
            vm((128, 256), BF16),
            vm((16, HD), BF16),
            vm((16, HD), BF16),
        ),
        in_specs=[smem, smem, hbm, hbm, hbm, hbm],
        out_specs=(vmem, vmem, vmem),
        scratch_shapes=scratch,
        compiler_params=pltpu.CompilerParams(
            collective_id=0, has_side_effects=True, vmem_limit_bytes=60 * 1024 * 1024
        ),
    )(
        doc_lengths,
        span_order.T,
        queries,
        out_grad,
        key_rows.reshape(4, 2, 16, HD),
        value_rows.reshape(4, 2, 16, HD),
    )


def solution(mesh):
    in_specs = (P("ctx", "head"), P("ctx", None), P("ctx", None), P("ctx", "head"), P(), P())
    out_specs = (P("ctx", "head"), P(("ctx", "head"), None), P(("ctx", "head"), None))
    return jax.shard_map(local, mesh=mesh, in_specs=in_specs, out_specs=out_specs, check_vma=False)
```

time: 61.7 us -> 53 us (0.86)
  Pallas kernels: 58.5 us -> 49.8 us
    pallas_call x1, Pallas kernels: 58.5 us -> 49.8 us  [local(): pl.pallas_call(kernel, out_shape=(vm((128, 256), BF16), vm((16, HD), BF16...]
where the time goes in v3:
time: 53 us; the launch traced here: 52.3 us
  Pallas kernels  49.8 us (94%)
  local copies, waits for them, and re-layouts  1.82 us (3%)
  between operations  0.64 us (1%)
    pallas_call x1, Pallas kernels, local(): pl.pallas_call(kernel, out_shape=(vm((128, 256), BF16), vm((16, HD), BF16...  49.8 us
    unnamed x3, local copies, waits for them, and re-layouts  1.82 us

profile of v3, /device:TPU:6, one launch (start us, length us, event | category | flops | bytes accessed | tf_op | source)
XLA Modules:
  0.0 52.3 jit_solution(14742216965681762302)
XLA Ops:
  0.6 49.8 %shard_map.85 = (bf16[128,256]{1,0:T(8,128)(2,1)S(1)}, bf16[16,128]{1,0:T(8,128)(2,1)S(1)}, bf16[16,128]{1,0:T(8,128)(2,1)S(1)}) custom-call(s32[8]{0:T(128)} %lens_ref.1, s32[2,64]{1,0:T(2,128)} %bitcast.5, bf16[128,256]{1,0:T(8,128)(2,1)} %q_ref.1, bf16[128,256]{1,0:T(8,128)(2,1)} %g_ref.1, bf16[4,2,16,128]{3,2,1,0:T(8,128)(2,1)} %bitcast.3, ...), custom_call_target="tpu_custom_call" | custom-call | tf_op jit(solution)/shard_map/pallas_call | solution.py:479
  50.5 0.6 %copy.12 = bf16[128,256]{1,0:T(8,128)(2,1)} copy(bf16[128,256]{1,0:T(8,128)(2,1)S(1)} %get-tuple-element.3) | data formatting | bytes 131072
  51.1 0.6 %copy.13 = bf16[16,128]{1,0:T(8,128)(2,1)} copy(bf16[16,128]{1,0:T(8,128)(2,1)S(1)} %get-tuple-element.4) | data formatting | bytes 8192
  51.7 0.6 %copy.14 = bf16[16,128]{1,0:T(8,128)(2,1)} copy(bf16[16,128]{1,0:T(8,128)(2,1)S(1)} %get-tuple-element.5) | data formatting | bytes 8192

commit v4 on v3

--- a/solution.py
+++ b/solution.py
@@ -70,7 +70,7 @@
         pl.semaphore_signal(sem, inc=1, device_id=dev, device_id_type=MESH)
 
     barrier = pltpu.get_barrier_semaphore()
-    peers = [odev, ydev[1], ydev[7], ydev[2], ydev[6], zout] + gdev[1:]
+    peers = [odev, zout] + [ydev[r] for r in (1, 7, 2, 6, 3, 5)] + gdev[1:]
     for p in peers:
         signal(barrier, p)
     pl.semaphore_wait(barrier, len(peers))
@@ -91,35 +91,33 @@
             device_id=odev, device_id_type=MESH,
         ).wait_recv()
 
-    def blk(i, c, r):
-        return kv.at[i, RPOS[r % 8], c]
+    def blk(c, r):
+        return kv.at[:, RPOS[r % 8], c]
 
     def x_forward(r):
         r = r % 8
-        for i in range(2):
-            send(blk(i, 0, r), blk(i, 1, r), xsend.at[r, i], xrecv.at[r, i], odev)
+        send(blk(0, r), blk(1, r), xsend.at[r], xrecv.at[r], odev)
 
     def x_landed(r):
         r = r % 8
-        for i in range(2):
-            landed(blk(i, 1, r), xsend.at[r, i], xrecv.at[r, i])
-
-    def y_send(i, src, dst, to, sem):
-        send(blk(i, 0, src), blk(i, 0, dst), ysend.at[sem, i], yrecv.at[sem, i], ydev[to])
-
-    def y_landed(i, r, sem):
-        landed(blk(i, 0, r), ysend.at[sem, i], yrecv.at[sem, i])
+        landed(blk(1, r), xsend.at[r], xrecv.at[r])
+
+    def y_send(r):
+        send(blk(0, 0), blk(0, -r), ysend.at[r], yrecv.at[r], ydev[r])
+
+    def y_landed(r):
+        landed(blk(0, r), ysend.at[(-r) % 8], yrecv.at[(-r) % 8])
+
+    def part(i, r):
+        return kv.at[i, RPOS[r], 0]
 
     stage[0].wait()
-    y_send(0, 0, 6, 2, 2)
-    y_send(0, 0, 2, 6, 6)
     stage[1].wait()
-    y_send(1, 0, 6, 2, 2)
-    y_send(1, 0, 2, 6, 6)
+    y_send(1)
+    y_send(7)
     x_forward(0)
-    for i in range(2):
-        y_send(i, 0, 7, 1, 1)
-        y_send(i, 0, 1, 7, 7)
+    for r in (2, 6, 3, 5):
+        y_send(r)
     for k in (2, 4, 1):
         send(q_ref, qa.at[k], qsend.at[k, 0], qrecv.at[k, 0], gdev[k])
         send(g_ref, ga.at[k], qsend.at[k, 1], qrecv.at[k, 1], gdev[k])
@@ -201,22 +199,16 @@
     q_landed(1)
     g_landed(1)
     units(0)
-    for i in range(2):
-        y_landed(i, 6, 2)
-        y_send(i, 6, 5, 1, 3)
-        if i == 0:
-            y_send(0, 6, 4, 2, 4)
-        y_landed(i, 2, 6)
-        y_send(i, 2, 3, 7, 5)
-        if i == 1:
-            y_send(1, 2, 4, 6, 4)
-    for i in range(2):
-        y_landed(i, 7, 1)
-        y_landed(i, 1, 7)
+    y_landed(7)
     x_forward(7)
+    y_landed(1)
     x_forward(1)
+    y_landed(6)
+    send(part(0, 6), part(0, 4), ysend.at[4], yrecv.at[4], ydev[2])
+    x_forward(6)
+    y_landed(2)
+    send(part(1, 2), part(1, 4), ysend.at[0], yrecv.at[0], ydev[6])
     x_forward(2)
-    x_forward(6)
     q_landed(2)
     q_pass(2, 6, gdev[4])
     q_pass(2, 3, gdev[1])
@@ -233,14 +225,12 @@
     pl.semaphore_wait(nearsem.at[1], 1)
     signal(nearsem.at[2], zdev[3])
     pass1(0, 0)
-    for i in range(2):
-        y_landed(i, 5, 3)
+    y_landed(5)
     x_forward(5)
-    for i in range(2):
-        y_landed(i, 3, 5)
+    y_landed(3)
     x_forward(3)
-    y_landed(0, 4, 4)
-    y_landed(1, 4, 4)
+    landed(part(0, 4), ysend.at[4], yrecv.at[4])
+    landed(part(1, 4), ysend.at[0], yrecv.at[0])
     x_forward(4)
     q_landed(6)
     q_pass(6, 7, gdev[1])
@@ -371,9 +361,9 @@
     send(yb.at[4, 1], yr.at[4, 1], rysend.at[0], ryrecv.at[0], ydev[6])
     block(0, 0, 2, False)
     yb[5] = column_sum(5).astype(BF16)
-    y_out(5, 7)
+    y_out(5, 5)
     yb[3] = column_sum(3).astype(BF16)
-    y_out(3, 1)
+    y_out(3, 3)
 
     def dq_part(k, h, hd):
         o = ((k // 2) * 2 + h) * UQ + ((k % 2) * 2 + hd) * 64
@@ -389,22 +379,20 @@
 
     t6 = column_sum(6)
     t2 = column_sum(2)
-    y_in(5)
     landed(yr.at[4, 1], rysend.at[0], ryrecv.at[0])
-    yb[6, 0] = (t6[0] + yr[5, 0].astype(F32)).astype(BF16)
-    yb[6, 1] = (t6[1] + yr[5, 1].astype(F32) + yr[4, 1].astype(F32)).astype(BF16)
+    yb[6, 0] = t6[0].astype(BF16)
+    yb[6, 1] = (t6[1] + yr[4, 1].astype(F32)).astype(BF16)
     y_out(6, 6)
-    y_in(3)
     landed(yr.at[4, 0], rysend.at[4], ryrecv.at[4])
-    yb[2, 0] = (t2[0] + yr[3, 0].astype(F32) + yr[4, 0].astype(F32)).astype(BF16)
-    yb[2, 1] = (t2[1] + yr[3, 1].astype(F32)).astype(BF16)
+    yb[2, 0] = (t2[0] + yr[4, 0].astype(F32)).astype(BF16)
+    yb[2, 1] = t2[1].astype(BF16)
     y_out(2, 2)
     yb[1] = column_sum(1).astype(BF16)
     y_out(1, 1)
     yb[7] = column_sum(7).astype(BF16)
     y_out(7, 7)
     own = column_sum(0)
-    for r in (1, 7, 2, 6):
+    for r in (5, 3, 1, 6, 2, 7):
         y_in(r)
         own = own + yr[r].astype(F32)
     pf[0, :, 0] = own
@@ -464,8 +452,8 @@
         vm((4, 2, 16, HD), BF16),
         dma((4,)),
         dma((8, 2)), dma((8, 2)),
-        dma((8, 2)), dma((8, 2)),
-        dma((8, 2)), dma((8, 2)),
+        dma((8,)), dma((8,)),
+        dma((8,)), dma((8,)),
         dma((8, 2)), dma((8, 2)),
         dma((8,)), dma((8,)),
         dma((8,)), dma((8,)),

time: 53 us -> 53 us (level)
  the two profiles are of different devices: /device:TPU:6 before, /device:TPU:2 now
where the time goes in v4:
time: 53 us; the launch traced here: 52.9 us
  Pallas kernels  50.4 us (95%)
  local copies, waits for them, and re-layouts  1.82 us (3%)
  between operations  0.64 us (1%)
    pallas_call x1, Pallas kernels, local(): pl.pallas_call(kernel, out_shape=(vm((128, 256), BF16), vm((16, HD), BF16...  50.4 us
    unnamed x3, local copies, waits for them, and re-layouts  1.82 us

profile of v4, /device:TPU:2, one launch (start us, length us, event | category | flops | bytes accessed | tf_op | source)
XLA Modules:
  0.0 52.9 jit_solution(10524132363506174256)
XLA Ops:
  0.6 50.4 %shard_map.85 = (bf16[128,256]{1,0:T(8,128)(2,1)S(1)}, bf16[16,128]{1,0:T(8,128)(2,1)S(1)}, bf16[16,128]{1,0:T(8,128)(2,1)S(1)}) custom-call(s32[8]{0:T(128)} %lens_ref.1, s32[2,64]{1,0:T(2,128)} %bitcast.5, bf16[128,256]{1,0:T(8,128)(2,1)} %q_ref.1, bf16[128,256]{1,0:T(8,128)(2,1)} %g_ref.1, bf16[4,2,16,128]{3,2,1,0:T(8,128)(2,1)} %bitcast.3, ...), custom_call_target="tpu_custom_call" | custom-call | tf_op jit(solution)/shard_map/pallas_call | solution.py:467
  51.0 0.6 %copy.12 = bf16[128,256]{1,0:T(8,128)(2,1)} copy(bf16[128,256]{1,0:T(8,128)(2,1)S(1)} %get-tuple-element.3) | data formatting | bytes 131072
  51.7 0.6 %copy.13 = bf16[16,128]{1,0:T(8,128)(2,1)} copy(bf16[16,128]{1,0:T(8,128)(2,1)S(1)} %get-tuple-element.4) | data formatting | bytes 8192
  52.3 0.6 %copy.14 = bf16[16,128]{1,0:T(8,128)(2,1)} copy(bf16[16,128]{1,0:T(8,128)(2,1)S(1)} %get-tuple-element.5) | data formatting | bytes 8192

commit v5 on v4

--- a/solution.py
+++ b/solution.py
@@ -23,6 +23,8 @@
 
 
 def swap_rows(v, p):
+    if p == 0:
+        return v
     parts = [v[(k ^ p) * 2 : (k ^ p) * 2 + 2] for k in range(4)]
     return jnp.concatenate(parts, axis=0)
 
@@ -47,6 +49,7 @@
 
     odev = (at(zl, y, xo), head)
     ydev = [(at(zl, (y + r) % 8, x), head) for r in range(8)]
+    ddev = [(at(zl, (y + r) % 8, xo), head) for r in range(8)]
     zdev = [(ctx, ((zh + r) % 4) * 2 + core) for r in range(4)]
     gdev = [
         (
@@ -71,6 +74,7 @@
 
     barrier = pltpu.get_barrier_semaphore()
     peers = [odev, zout] + [ydev[r] for r in (1, 7, 2, 6, 3, 5)] + gdev[1:]
+    peers = peers + [ddev[r] for r in (1, 7, 2, 6)]
     for p in peers:
         signal(barrier, p)
     pl.semaphore_wait(barrier, len(peers))
@@ -105,19 +109,19 @@
     def y_send(r):
         send(blk(0, 0), blk(0, -r), ysend.at[r], yrecv.at[r], ydev[r])
 
-    def y_landed(r):
-        landed(blk(0, r), ysend.at[(-r) % 8], yrecv.at[(-r) % 8])
-
-    def part(i, r):
-        return kv.at[i, RPOS[r], 0]
+    def y_landed(i, r):
+        landed(blk(0, r), ysend.at[i], yrecv.at[i])
+
+    def part(i, r, c=0):
+        return kv.at[i, RPOS[r], c]
 
     stage[0].wait()
     stage[1].wait()
     y_send(1)
     y_send(7)
     x_forward(0)
-    for r in (2, 6, 3, 5):
-        y_send(r)
+    y_send(2)
+    y_send(6)
     for k in (2, 4, 1):
         send(q_ref, qa.at[k], qsend.at[k, 0], qrecv.at[k, 0], gdev[k])
         send(g_ref, ga.at[k], qsend.at[k, 1], qrecv.at[k, 1], gdev[k])
@@ -199,16 +203,22 @@
     q_landed(1)
     g_landed(1)
     units(0)
-    y_landed(7)
+    y_landed(1, 7)
     x_forward(7)
-    y_landed(1)
+    y_landed(7, 1)
     x_forward(1)
-    y_landed(6)
+    y_landed(2, 6)
+    send(blk(0, 6), blk(0, 5), ysend.at[3], yrecv.at[3], ydev[1])
     send(part(0, 6), part(0, 4), ysend.at[4], yrecv.at[4], ydev[2])
     x_forward(6)
-    y_landed(2)
+    send(blk(0, 6), blk(1, 5), xsend.at[5], xrecv.at[5], ddev[1])
+    send(part(0, 6), part(0, 4, 1), xsend.at[4], xrecv.at[4], ddev[2])
+    y_landed(6, 2)
+    send(blk(0, 2), blk(0, 3), ysend.at[5], yrecv.at[5], ydev[7])
     send(part(1, 2), part(1, 4), ysend.at[0], yrecv.at[0], ydev[6])
     x_forward(2)
+    send(blk(0, 2), blk(1, 3), xsend.at[3], xrecv.at[3], ddev[7])
+    send(part(1, 2), part(1, 4, 1), xsend.at[8], xrecv.at[8], ddev[6])
     q_landed(2)
     q_pass(2, 6, gdev[4])
     q_pass(2, 3, gdev[1])
@@ -225,13 +235,10 @@
     pl.semaphore_wait(nearsem.at[1], 1)
     signal(nearsem.at[2], zdev[3])
     pass1(0, 0)
-    y_landed(5)
-    x_forward(5)
-    y_landed(3)
-    x_forward(3)
+    y_landed(3, 5)
+    y_landed(5, 3)
     landed(part(0, 4), ysend.at[4], yrecv.at[4])
     landed(part(1, 4), ysend.at[0], yrecv.at[0])
-    x_forward(4)
     q_landed(6)
     q_pass(6, 7, gdev[1])
     g_landed(6)
@@ -259,7 +266,8 @@
     for g in range(4):
         pass1(2, g)
     x_landed(5)
-    x_landed(4)
+    landed(part(0, 4, 1), xsend.at[4], xrecv.at[4])
+    landed(part(1, 4, 1), xsend.at[8], xrecv.at[8])
     def top(vals):
         while len(vals) > 1:
             vals = [jnp.maximum(a, b) for a, b in zip(vals[::2], vals[1::2])]
@@ -288,16 +296,23 @@
         rows = slice(dx * 8, dx * 8 + 8)
         for k in range(1, 8):
             landed(rst.at[k, dx], ssend.at[k, dx], srecv.at[k, dx])
-        got = [[st[dx, i]] + [swap_rows(rst[p, dx, i], p % 4) for p in range(1, 8)] for i in range(3)]
-        gm = top(got[0])
-        sc = [jnp.exp2((a - gm) * EXP_SCALE) for a in got[0]]
-        inv = 1.0 / sum(sc[p] * got[1][p] for p in range(8))
-        fac[4, rows] = sum(sc[p] * got[2][p] for p in range(8)) * inv
+        got = [[st[dx, i]] + [rst[p, dx, i] for p in range(1, 8)] for i in range(3)]
+        gm = top([swap_rows(jnp.maximum(got[0][p], got[0][p + 4]), p) for p in range(4)])
+        total, dot = None, None
+        for p in range(4):
+            back = swap_rows(gm, p)
+            a = jnp.exp2((got[0][p] - back) * EXP_SCALE)
+            b = jnp.exp2((got[0][p + 4] - back) * EXP_SCALE)
+            l = swap_rows(a * got[1][p] + b * got[1][p + 4], p)
+            d = swap_rows(a * got[2][p] + b * got[2][p + 4], p)
+            total = l if total is None else total + l
+            dot = d if dot is None else dot + d
+        inv = 1.0 / total
+        fac[4, rows] = dot * inv
         for j in range(4):
             fac[j, rows] = jnp.exp2((stm[j, 0, rows] - gm) * EXP_SCALE) * inv
 
-    def block(c, j0, nj, first):
-        nk = nj * 128
+    def elements(c, j0, nj):
         for u in range(NU):
             g, h = u // 2, u % 2
             for dc in range(2):
@@ -311,23 +326,41 @@
                     w = es[j, u, ko : ko + 64, cols] * fac[j, row : row + 1, :]
                     ws[i * 64 : i * 64 + 64, o : o + HD] = w.astype(BF16)
                     d = w * (dps[j, u, ko : ko + 64, cols] - delta)
-                    dss[i * 64 : i * 64 + 64, o : o + HD] = d.astype(BF16)
+                    ro = j0 * 128 + i * 64
+                    dss[c, ro : ro + 64, o : o + HD] = d.astype(BF16)
+
+    def key_part(c, j0, nj):
         dims = (((1,), (0,)), ((), ()))
         q_all = qs[...].reshape(NU * UQ, HD)
         g_all = gs[...].reshape(NU * UQ, HD)
-        r0, n = 2 * j0, 2 * nj
-        dkc = lax.dot_general(dss[0:nk], q_all, dims, preferred_element_type=F32)
+        nk, r0, n = nj * 128, 2 * j0, 2 * nj
+        ko = j0 * 128
+        dkc = lax.dot_general(dss[c, ko : ko + nk], q_all, dims, preferred_element_type=F32)
         pf[c, 0, r0 : r0 + n] = dkc.reshape(n, 64, HD)
         dvc = lax.dot_general(ws[0:nk], g_all, dims, preferred_element_type=F32)
         pf[c, 1, r0 : r0 + n] = dvc.reshape(n, 64, HD)
-        keys = kv[0, r0 : r0 + n, c].reshape(nk, HD)
-        add = lax.dot_general(
-            dss[0:nk], keys, (((0,), (0,)), ((), ())), preferred_element_type=F32
-        )
-        if first:
-            dqa[...] = add
-        else:
-            dqa[...] += add
+
+    def query_part(g):
+        dims = (((0,), (0,)), ((), ()))
+        o = g * 2 * UQ
+        t = None
+        for c in range(2):
+            keys = kv[0, :, c].reshape(512, HD)
+            a = lax.dot_general(
+                dss[c, :, o : o + 2 * UQ], keys, dims, preferred_element_type=F32
+            )
+            t = a if t is None else t + a
+        dqa[...] = t
+        for dc in range(2):
+            k = g * 2 + dc
+            if k > 0:
+                for h in range(2):
+                    for hd in range(2):
+                        rows = slice(h * 64, h * 64 + 64)
+                        cols = slice(hd * HD, hd * HD + HD)
+                        a = h * UQ + (dc * 2 + hd) * 64
+                        dqb[k, rows, cols] = dqa[a : a + 64, :].astype(BF16)
+                send(dqb.at[k], dqr.at[k], dsend.at[k], drecv.at[k], gdev[k])
 
     def mine(c, r):
         return pf[c, :, RPOS[r]]
@@ -346,36 +379,33 @@
     def y_in(r):
         landed(yr.at[r], rysend.at[r], ryrecv.at[r])
 
-    block(1, 3, 1, True)
+    elements(1, 3, 1)
+    key_part(1, 3, 1)
     x_send(4)
     x_send(5)
-    block(1, 2, 1, False)
+    elements(1, 2, 1)
+    key_part(1, 2, 1)
     x_send(3)
     x_send(6)
-    block(0, 2, 2, False)
-    block(1, 0, 2, False)
+    elements(1, 0, 2)
+    key_part(1, 0, 2)
     for r in (2, 1, 7, 0):
         x_send(r)
+    elements(0, 2, 2)
+    key_part(0, 2, 2)
     yb[4] = column_sum(4).astype(BF16)
     send(yb.at[4, 0], yr.at[4, 0], rysend.at[4], ryrecv.at[4], ydev[2])
     send(yb.at[4, 1], yr.at[4, 1], rysend.at[0], ryrecv.at[0], ydev[6])
-    block(0, 0, 2, False)
+    elements(0, 0, 2)
+    query_part(3)
+    query_part(2)
     yb[5] = column_sum(5).astype(BF16)
     y_out(5, 5)
     yb[3] = column_sum(3).astype(BF16)
     y_out(3, 3)
-
-    def dq_part(k, h, hd):
-        o = ((k // 2) * 2 + h) * UQ + ((k % 2) * 2 + hd) * 64
-        return dqa[o : o + 64, :]
-
-    for k in (6, 7, 4, 5, 2, 3, 1):
-        for h in range(2):
-            for hd in range(2):
-                rows = slice(h * 64, h * 64 + 64)
-                cols = slice(hd * HD, hd * HD + HD)
-                dqb[k, rows, cols] = dq_part(k, h, hd).astype(BF16)
-        send(dqb.at[k], dqr.at[k], dsend.at[k], drecv.at[k], gdev[k])
+    query_part(1)
+    query_part(0)
+    key_part(0, 0, 2)
 
     t6 = column_sum(6)
     t2 = column_sum(2)
@@ -407,7 +437,8 @@
         for hd in range(2):
             rows = slice(h * 64, h * 64 + 64)
             cols = slice(hd * HD, hd * HD + HD)
-            t = dq_part(0, h, hd)
+            o = h * UQ + hd * 64
+            t = dqa[o : o + 64, :]
             for k in range(1, 8):
                 t = t + dqr[k, rows, cols].astype(F32)
             dq_ref[rows, cols] = (t * SCALE).astype(BF16)
@@ -435,8 +466,8 @@
         vm((4, NU, CK, UQ), F32),
         vm((4, NU, CK, UQ), F32),
         vm((CK, NU * UQ), BF16),
-        vm((CK, NU * UQ), BF16),
-        vm((NU * UQ, HD), F32),
+        vm((2, 512, NU * UQ), BF16),
+        vm((2 * UQ, HD), F32),
         vm((2, 2, 8, 64, HD), F32),
         vm((4, 3, 16, HD), F32),
         vm((2, 3, 8, HD), F32),
@@ -453,7 +484,7 @@
         dma((4,)),
         dma((8, 2)), dma((8, 2)),
         dma((8,)), dma((8,)),
-        dma((8,)), dma((8,)),
+        dma((9,)), dma((9,)),
         dma((8, 2)), dma((8, 2)),
         dma((8,)), dma((8,)),
         dma((8,)), dma((8,)),

time: 53 us -> 52.1 us (0.983)
  the two profiles are of different devices: /device:TPU:2 before, /device:TPU:6 now
where the time goes in v5:
time: 52.1 us; the launch traced here: 51.5 us
  Pallas kernels  49.1 us (94%)
  local copies, waits for them, and re-layouts  1.82 us (3%)
  between operations  0.64 us (1%)
    pallas_call x1, Pallas kernels, local(): pl.pallas_call(kernel, out_shape=(vm((128, 256), BF16), vm((16, HD), BF16...  49.1 us
    unnamed x3, local copies, waits for them, and re-layouts  1.82 us

profile of v5, /device:TPU:6, one launch (start us, length us, event | category | flops | bytes accessed | tf_op | source)
XLA Modules:
  0.0 51.5 jit_solution(870930399145562687)
XLA Ops:
  0.6 49.1 %shard_map.85 = (bf16[128,256]{1,0:T(8,128)(2,1)S(1)}, bf16[16,128]{1,0:T(8,128)(2,1)S(1)}, bf16[16,128]{1,0:T(8,128)(2,1)S(1)}) custom-call(s32[8]{0:T(128)} %lens_ref.1, s32[2,64]{1,0:T(2,128)} %bitcast.5, bf16[128,256]{1,0:T(8,128)(2,1)} %q_ref.1, bf16[128,256]{1,0:T(8,128)(2,1)} %g_ref.1, bf16[4,2,16,128]{3,2,1,0:T(8,128)(2,1)} %bitcast.3, ...), custom_call_target="tpu_custom_call" | custom-call | tf_op jit(solution)/shard_map/pallas_call | solution.py:498
  49.7 0.6 %copy.12 = bf16[128,256]{1,0:T(8,128)(2,1)} copy(bf16[128,256]{1,0:T(8,128)(2,1)S(1)} %get-tuple-element.3) | data formatting | bytes 131072
  50.3 0.6 %copy.13 = bf16[16,128]{1,0:T(8,128)(2,1)} copy(bf16[16,128]{1,0:T(8,128)(2,1)S(1)} %get-tuple-element.4) | data formatting | bytes 8192
  50.9 0.6 %copy.14 = bf16[16,128]{1,0:T(8,128)(2,1)} copy(bf16[16,128]{1,0:T(8,128)(2,1)S(1)} %get-tuple-element.5) | data formatting | bytes 8192

commit v6 on v5

--- a/solution.py
+++ b/solution.py
@@ -198,11 +198,6 @@
     def g_pass(k, to, dev):
         send(ga.at[k], ga.at[to], qsend.at[to, 1], qrecv.at[to, 1], dev)
 
-    stage[2].wait()
-    stage[3].wait()
-    q_landed(1)
-    g_landed(1)
-    units(0)
     y_landed(1, 7)
     x_forward(7)
     y_landed(7, 1)
@@ -229,6 +224,11 @@
     g_pass(4, 5, gdev[1])
     g_landed(2)
     g_pass(2, 3, gdev[1])
+    stage[2].wait()
+    stage[3].wait()
+    q_landed(1)
+    g_landed(1)
+    units(0)
     x_landed(0)
     x_landed(1)
     pl.semaphore_wait(nearsem.at[0], 1)

time: 52.1 us -> 52.1 us (level)
  no operation moved by 1% of the time
where the time goes in v6:
time: 52.1 us; the launch traced here: 51.5 us
  Pallas kernels  49.1 us (94%)
  local copies, waits for them, and re-layouts  1.82 us (3%)
  between operations  0.64 us (1%)
    pallas_call x1, Pallas kernels, local(): pl.pallas_call(kernel, out_shape=(vm((128, 256), BF16), vm((16, HD), BF16...  49.1 us
    unnamed x3, local copies, waits for them, and re-layouts  1.82 us

profile of v6, /device:TPU:6, one launch (start us, length us, event | category | flops | bytes accessed | tf_op | source)
XLA Modules:
  0.0 51.5 jit_solution(5196340428261087602)
XLA Ops:
  0.6 49.1 %shard_map.85 = (bf16[128,256]{1,0:T(8,128)(2,1)S(1)}, bf16[16,128]{1,0:T(8,128)(2,1)S(1)}, bf16[16,128]{1,0:T(8,128)(2,1)S(1)}) custom-call(s32[8]{0:T(128)} %lens_ref.1, s32[2,64]{1,0:T(2,128)} %bitcast.5, bf16[128,256]{1,0:T(8,128)(2,1)} %q_ref.1, bf16[128,256]{1,0:T(8,128)(2,1)} %g_ref.1, bf16[4,2,16,128]{3,2,1,0:T(8,128)(2,1)} %bitcast.3, ...), custom_call_target="tpu_custom_call" | custom-call | tf_op jit(solution)/shard_map/pallas_call | solution.py:498
  49.7 0.6 %copy.12 = bf16[128,256]{1,0:T(8,128)(2,1)} copy(bf16[128,256]{1,0:T(8,128)(2,1)S(1)} %get-tuple-element.3) | data formatting | bytes 131072
  50.3 0.6 %copy.13 = bf16[16,128]{1,0:T(8,128)(2,1)} copy(bf16[16,128]{1,0:T(8,128)(2,1)S(1)} %get-tuple-element.4) | data formatting | bytes 8192
  50.9 0.6 %copy.14 = bf16[16,128]{1,0:T(8,128)(2,1)} copy(bf16[16,128]{1,0:T(8,128)(2,1)S(1)} %get-tuple-element.5) | data formatting | bytes 8192
